TPU v7x, 32 devices: a whole 2x2x4 slice. The times are simulated.
32 devices in a mesh: grp: 2 (over y), blk: 4 (over z), bulk: 4 (over x, core).
Axes of the slice: x: 2, y: 2, z: 4, core: 2. Of those that a mesh axis runs over, the one named last changes fastest.
Arguments:
- tokens: bfloat16 [80, 8192], P(('grp', 'blk'), 'bulk'), parts along dimension 0, may hold values from -6 to 6
- cotangent: bfloat16 [80, 8192], P(('grp', 'blk'), 'bulk'), parts along dimension 0, may hold values from -1.5 to 1.5
- gate_weight: bfloat16 [8192, 26624], P('bulk', 'blk'), may hold values from -0.0625 to 0.0625
- up_weight: bfloat16 [8192, 26624], P('bulk', 'blk'), may hold values from -0.0625 to 0.0625
- down_weight: bfloat16 [26624, 8192], P('blk', 'bulk'), may hold values from -0.0390625 to 0.0390625
Outputs:
- mixed: bfloat16 [80, 8192], P(('grp', 'blk'), 'bulk'), parts along dimension 0
- grad_input: bfloat16 [80, 8192], P(('grp', 'blk'), 'bulk'), parts along dimension 0
There are 2 independent parts, one for each index of `grp`. A program takes and returns all parts, laid end to end along the dimension named above; an argument that names none is the same for every part. Nothing has to cross between parts.
All inputs are finite; a program needn't handle non-finite values.
Results may differ from a plain program's by a relative error of at most 0.0049.
Values may be sent and summed in bfloat16 or wider, within the bound.
A program may use at most 192 MiB of HBM per device.

v0:
```python
import functools

import jax
import jax.numpy as jnp
from jax import lax
from jax.experimental import pallas as pl
from jax.experimental.pallas import tpu as pltpu
from jax.sharding import PartitionSpec as P

MESH = pl.DeviceIdType.MESH
BF = jnp.bfloat16
F32 = jnp.float32

AHEAD = 20
RING = 3
LAG = 4
def lags(n):
    return (1, 3, 5, 9, 10, 15) if n >= 24 else (1, 3, 4, 7, 8, 11)


NT = (((1,), (1,)), ((), ()))


def kernel(nb, nu, n, fc, tok_in, cot_in, wg_hbm, wu_hbm, wd_hbm, out,
           wg, wu, wd, own, tok_g, cot_g, tok, cot, part, pair, chip, far, act, mixed, grad, stage, zbuf,
           g_sem, u_sem, d_sem, tk_send, tk_recv, p_send, p_recv, f_send, f_recv,
           a_send, a_recv, fw_send, z_send, z_recv):
    S1, S2, S3, S4, S5, S6 = lags(n)
    b_me = lax.axis_index("blk")
    u_me = lax.axis_index("bulk")
    x_me, k_me = u_me // 2, u_me % 2
    chips = nu // 2
    rows = tok_in.shape[0]
    dh = grad.shape[2]
    partner = x_me * 2 + (1 - k_me)

    def load_gu(c):
        cols = pl.ds(pl.multiple_of(c * fc, fc), fc)
        return (pltpu.make_async_copy(wg_hbm.at[:, cols], wg.at[c], g_sem.at[c]),
                pltpu.make_async_copy(wu_hbm.at[:, cols], wu.at[c], u_sem.at[c]))

    def load_d(m):
        m = jnp.int32(m)
        c = lax.rem(m, n)
        slot = lax.rem(m, RING)
        return pltpu.make_async_copy(
            wd_hbm.at[pl.ds(pl.multiple_of(c * fc, fc), fc), :], wd.at[slot], d_sem.at[slot])

    ahead = min(AHEAD, n)
    lag = min(LAG, n - S6)
    keep = part.shape[0]
    many = 2 if n % 2 == 0 else 1
    for c in range(ahead):
        for cp in load_gu(c):
            cp.start()
        if c < RING:
            load_d(c).start()

    own[...] = jnp.zeros_like(own)
    own[0, :rows, :] = tok_in[...]
    own[1, :rows, :] = cot_in[...]
    stage[...] = jnp.zeros_like(stage)

    barrier = pltpu.get_barrier_semaphore()
    for d in range(1, nb):
        pl.semaphore_signal(barrier, inc=1, device_id={"blk": (b_me + d) % nb}, device_id_type=MESH)
    for d in range(1, nu):
        pl.semaphore_signal(barrier, inc=1, device_id={"bulk": (u_me + d) % nu}, device_id_type=MESH)
    pl.semaphore_wait(barrier, nb + nu - 2)

    def rcopy(src, dst, ss, rs, where):
        return pltpu.make_async_remote_copy(
            src_ref=src, dst_ref=dst, send_sem=ss, recv_sem=rs, device_id=where, device_id_type=MESH)

    def tok_copy(w, d):
        dst = tok_g if w == 0 else cot_g
        return rcopy(own.at[w], dst.at[d - 1], tk_send.at[w, d - 1], tk_recv.at[w, d - 1],
                     {"blk": (b_me + d) % nb})

    for w in range(2):
        for d in range(1, nb):
            tok_copy(w, d).start()

    def gather(w):
        src, got, dst = (tok_in, tok_g, tok) if w == 0 else (cot_in, cot_g, cot)
        for d in range(1, nb):
            tok_copy(w, d).wait_recv()
        for h in range(2):
            cols = pl.ds(h * dh, dh)
            for b in range(nb):
                slot = (b_me - b + nb) % nb
                other = got[jnp.maximum(slot - 1, 0), :rows, cols].astype(F32)
                mine = src[:, cols].astype(F32)
                mixed[h, pl.ds(b * rows, rows), :] = jnp.where(slot == 0, mine, other)
        for h in range(2):
            dst[:, h * dh:(h + 1) * dh] = mixed[h].astype(BF)

    def owner(c):
        o = lax.rem(c, nu)
        return o, lax.div(o, 2), lax.rem(o, 2)

    def pair_copy(c):
        return rcopy(part.at[lax.rem(c, keep)], pair.at[lax.div(c, 2)], p_send.at[c], p_recv.at[lax.div(c, 2)], {"bulk": partner})

    def far_copy(c):
        o, ox, ok = owner(c)
        slot = (x_me - ox + chips - 1 + chips) % chips
        return rcopy(chip.at[lax.div(c, 2)], far.at[lax.div(c, nu), slot], f_send.at[lax.div(c, 2)],
                     f_recv.at[lax.div(c, nu), slot], {"bulk": o})

    def far_wait(c, slot):
        rcopy(chip.at[lax.div(c, 2)], far.at[lax.div(c, nu), slot], f_send.at[lax.div(c, 2)],
              f_recv.at[lax.div(c, nu), slot], {"bulk": partner}).wait_recv()

    def act_copy(c, d):
        to = partner if d == 0 else ((x_me + d) % chips) * 2 + k_me
        return rcopy(act.at[c], act.at[c], a_send.at[lax.div(c, nu), d], a_recv.at[c], {"bulk": to})

    def forward(c):
        return rcopy(act.at[c], act.at[c], fw_send.at[lax.div(c, 2)], a_recv.at[c], {"bulk": partner})

    def valid(c):
        return jnp.logical_and(c >= 0, c < n)

    def stages(i):
        c1 = i - S1

        @pl.when(jnp.logical_and(valid(c1), owner(c1 + nu)[2] != k_me))
        def _():
            pair_copy(c1).start()

        c3 = i - S3
        o3 = owner(c3 + nu)

        @pl.when(jnp.logical_and(valid(c3), jnp.logical_and(o3[2] == k_me, o3[1] != x_me)))
        def _():
            far_copy(c3).start()

        c5 = i - S5

        @pl.when(jnp.logical_and(valid(c5), owner(c5 + nu)[0] == u_me))
        def _():
            for d in range(chips):
                act_copy(c5, d).start()

        c6 = i - S6
        o6 = owner(c6 + nu)

        @pl.when(jnp.logical_and(valid(c6), jnp.logical_and(o6[2] == k_me, o6[1] != x_me)))
        def _():
            forward(c6).wait_recv()
            forward(c6).start()

        c2 = i - S2
        o2 = owner(c2 + nu)

        @pl.when(jnp.logical_and(valid(c2), o2[2] == k_me))
        def _():
            pair_copy(c2).wait_recv()

            @pl.when(o2[1] != x_me)
            def _():
                for j in range(3):
                    chip[lax.div(c2, 2), j] = (
                        part[lax.rem(c2, keep), j] + pair[lax.div(c2, 2), j]).astype(BF)

        c4 = i - S4

        @pl.when(jnp.logical_and(valid(c4), owner(c4 + nu)[2] != k_me))
        def _():
            pair_copy(c4).wait_send()

        @pl.when(jnp.logical_and(valid(c4), owner(c4 + nu)[0] == u_me))
        def _():
            for slot in range(chips - 1):
                far_wait(c4, slot)

            def total(j):
                s = part[lax.rem(c4, keep), j] + pair[lax.div(c4, 2), j]
                for slot in range(chips - 1):
                    s = s + far[lax.div(c4, nu), slot, j].astype(F32)
                return s

            gate, upward, back = total(0), total(1), total(2)
            sigma = 1.0 / (1.0 + jnp.exp(-gate))
            act[c4, 0] = (gate * sigma * upward).astype(BF)
            act[c4, 1] = (back * upward * sigma * (1.0 + gate * (1.0 - sigma))).astype(BF)
            act[c4, 2] = (back * gate * sigma).astype(BF)

    def first(gu, back, i, _):
        m = i - lag
        stages(m)
        if gu:
            @pl.when(i + ahead < n)
            def _():
                for cp in load_gu(i + ahead):
                    cp.start()

            for cp in load_gu(i):
                cp.wait()
        if back:
            load_d(m).wait()
        if gu:
            part[lax.rem(i, keep), 0] = jnp.dot(tok[...], wg[i], preferred_element_type=F32)
            part[lax.rem(i, keep), 1] = jnp.dot(tok[...], wu[i], preferred_element_type=F32)
        if back:
            part[lax.rem(m, keep), 2] = lax.dot_general(
                cot[...], wd[lax.rem(m, RING)], NT, preferred_element_type=F32)
            load_d(m + RING).start()
        return 0

    gather(0)
    lax.fori_loop(0, lag, functools.partial(first, True, False), 0)
    gather(1)
    lax.fori_loop(lag, n, functools.partial(first, True, True), 0)
    lax.fori_loop(n, n + lag, functools.partial(first, False, True), 0)

    mixed[...] = jnp.zeros_like(mixed)
    grad[...] = jnp.zeros_like(grad)

    def add_grad(h, c):
        grad[h] += (
            lax.dot_general(act[c, 1], wg[c, h * dh:(h + 1) * dh, :], NT,
                            preferred_element_type=F32)
            + lax.dot_general(act[c, 2], wu[c, h * dh:(h + 1) * dh, :], NT,
                              preferred_element_type=F32))

    def second(j, _):
        m = j + n
        stages(m)

        @pl.when(owner(j)[2] != k_me)
        def _():
            forward(j).wait_recv()

        load_d(m).wait()
        add_grad(0, j)
        for h in range(2):
            mixed[h] += jnp.dot(
                act[j, 0], wd[lax.rem(m, RING), :, h * dh:(h + 1) * dh], preferred_element_type=F32)

        @pl.when(m + RING < 2 * n)
        def _():
            load_d(m + RING).start()

        return 0

    lax.fori_loop(0, n, second, 0)

    def z_stage(q):
        acc = mixed if q < 2 else grad
        for b in range(nb):
            stage[q, b, :rows, :] = acc[q % 2, b * rows:(b + 1) * rows, :].astype(BF)

    def z_copy(q, d):
        to = (b_me + d) % nb
        return rcopy(stage.at[q, to], zbuf.at[q, d - 1], z_send.at[q, d - 1], z_recv.at[q, d - 1],
                     {"blk": to})

    def z_send_all(q):
        for d in range(1, nb):
            z_copy(q, d).start()

    def z_finish(q):
        acc = mixed if q < 2 else grad
        h = q % 2
        s = jnp.zeros((rows, dh), F32)
        for b in range(nb):
            s = s + jnp.where(b == b_me, acc[h, b * rows:(b + 1) * rows, :], 0.0)
        for d in range(1, nb):
            z_copy(q, d).wait_recv()
            s = s + zbuf[q, d - 1, :rows, :].astype(F32)
        out[q // 2, :, h * dh:(h + 1) * dh] = s

    for q in range(3):
        z_stage(q)

    def third(c, _):
        @pl.when(c == 1)
        def _():
            for q in range(3):
                z_send_all(q)

        for k in range(many):
            add_grad(1, c * many + k)
        return 0

    lax.fori_loop(0, n // many, third, 0)
    z_stage(3)
    z_finish(0)
    z_send_all(3)
    z_finish(1)
    z_finish(2)

    for d in range(1, nb):
        for w in range(2):
            tok_copy(w, d).wait_send()

    def drain(c, _):
        o, ox, ok = owner(c)

        @pl.when(jnp.logical_and(ok == k_me, ox != x_me))
        def _():
            far_copy(c).wait_send()
            forward(c).wait_send()

        @pl.when(o == u_me)
        def _():
            for d in range(chips):
                act_copy(c, d).wait_send()

        return 0

    lax.fori_loop(0, n, drain, 0)
    z_finish(3)
    for q in range(4):
        for d in range(1, nb):
            z_copy(q, d).wait_send()


def per_device(nb, nu, tokens, cotangent, gate_weight, up_weight, down_weight):
    rows, depth = tokens.shape
    width = gate_weight.shape[1]
    fc = next(w for w in (256, 128) if width % w == 0)
    n = width // fc
    S4, S6 = lags(n)[3], lags(n)[5]
    assert n >= S6 and depth % 256 == 0 and nu % 2 == 0
    t = rows * nb
    tile = pl.cdiv(rows, 16) * 16
    dh = depth // 2
    owned = pl.cdiv(n, nu)
    halfn = pl.cdiv(n, 2)
    chips = nu // 2
    dma = pltpu.SemaphoreType.DMA
    vm = pltpu.VMEM
    both = pl.pallas_call(
        functools.partial(kernel, nb, nu, n, fc),
        out_shape=jax.ShapeDtypeStruct((2, rows, depth), F32),
        in_specs=[pl.BlockSpec(memory_space=pltpu.VMEM)] * 2 + [pl.BlockSpec(memory_space=pl.ANY)] * 3,
        out_specs=pl.BlockSpec(memory_space=pltpu.VMEM),
        scratch_shapes=[
            vm((n, depth, fc), BF), vm((n, depth, fc), BF), vm((RING, fc, depth), BF),
            vm((2, tile, depth), BF), vm((nb - 1, tile, depth), BF), vm((nb - 1, tile, depth), BF),
            vm((t, depth), BF), vm((t, depth), BF),
            vm((S4 + min(LAG, n - S6), 3, t, fc), F32), vm((halfn, 3, t, fc), F32), vm((halfn, 3, t, fc), BF), vm((owned, chips - 1, 3, t, fc), BF),
            vm((n, 3, t, fc), BF),
            vm((2, t, dh), F32), vm((2, t, dh), F32),
            vm((4, nb, tile, dh), BF), vm((4, nb - 1, tile, dh), BF),
            dma((n,)), dma((n,)), dma((RING,)),
            dma((2, nb - 1)), dma((2, nb - 1)),
            dma((n,)), dma((halfn,)), dma((halfn,)), dma((owned, chips - 1)),
            dma((owned, chips)), dma((n,)), dma((halfn,)),
            dma((4, nb - 1)), dma((4, nb - 1)),
        ],
        compiler_params=pltpu.CompilerParams(
            collective_id=0, has_side_effects=True, vmem_limit_bytes=67043328),
    )(tokens, cotangent, gate_weight, up_weight, down_weight)
    return both[0].astype(BF), both[1].astype(BF)


def solution(mesh):
    return jax.shard_map(
        functools.partial(per_device, mesh.shape["blk"], mesh.shape["bulk"]),
        mesh=mesh,
        in_specs=(
            P(("grp", "blk"), "bulk"),
            P(("grp", "blk"), "bulk"),
            P("bulk", "blk"),
            P("bulk", "blk"),
            P("blk", "bulk"),
        ),
        out_specs=(P(("grp", "blk"), "bulk"), P(("grp", "blk"), "bulk")),
        check_vma=False,
    )
```

profile of v0, /device:TPU:0, one launch (start us, length us, event | category | flops | bytes accessed | tf_op | source)
XLA Modules:
  0.0 81.9 jit_solution(8778509553507227638)
XLA Ops:
  0.6 79.7 %shard_map.68 = f32[2,10,2048]{2,1,0:T(8,128)} custom-call(bf16[10,2048]{1,0:T(8,128)(2,1)} %tok_in.1, bf16[10,2048]{1,0:T(8,128)(2,1)} %cot_in.1, bf16[2048,6656]{1,0:T(8,128)(2,1)} %wg_hbm.1, bf16[2048,6656]{1,0:T(8,128)(2,1)} %wu_hbm.1, bf16[6656,2048]{1,0:T(8,128)(2,1)} %wd_hbm.1), custom_call_target="tpu_custom_call" | custom-call | tf_op jit(solution)/shard_map/pallas_call | solution.py:336
  80.3 1.0 %convert.4 = bf16[2,10,2048]{2,1,0:T(8,128)(2,1)S(1)} convert(f32[2,10,2048]{2,1,0:T(8,128)} %shard_map.68) | non-fusion elementwise | flops 40960 | bytes 245760 | tf_op jit(solution)/shard_map/convert.1
  81.3 0.7 slice_bitcast_fusion
where the time goes:
time: 82.1 us; the launch traced here: 81.9 us
  Pallas kernels  79.7 us (97%)
  other arithmetic  0.97 us (1%)
    pallas_call x1, Pallas kernels, per_device(): pl.pallas_call(functools.partial(kernel, nb, nu, n, fc), out_shape=jax.Sh...  79.7 us

commit v1 on v0

v1 whole, which is shorter than its diff:
```python
import functools

import jax
import jax.numpy as jnp
from jax import lax
from jax.experimental import pallas as pl
from jax.experimental.pallas import tpu as pltpu
from jax.sharding import PartitionSpec as P

MESH = pl.DeviceIdType.MESH
BF = jnp.bfloat16
F32 = jnp.float32
NT = (((1,), (1,)), ((), ()))
EARLY = 4
PARTS = 4


def flip(i, m):
    return i + m - 2 * m * ((i // m) % 2)


def kernel(nb, nu, n, total, fc, tok_in, cot_in, wg_hbm, wu_hbm, wd_hbm, out,
           wg, wu, wd, got, tok, cot, part, pair, chip, far, coef, act,
           mixed, grad, ysend, yrecv, ysum, zsend, zrecv,
           g_sem, u_sem, d_sem, own_sem, tk_send, tk_recv, p_send, p_recv,
           f_send, f_recv, a_send, a_recv, y_send, y_recv, z_send, z_recv):
    g_me = lax.axis_index("grp")
    b_me = lax.axis_index("blk")
    u_me = lax.axis_index("bulk")
    x_me, k_me = u_me // 2, u_me % 2
    chips = nu // 2
    rows, depth = tok_in.shape
    half = nb * rows
    pw = depth // PARTS
    steps = nb.bit_length() - 1
    bits = [1 << s for s in range(steps)]
    first_chunk = jnp.minimum(g_me * n, total - n)
    partner = {"bulk": x_me * 2 + (1 - k_me)}
    across = {"grp": 1 - g_me}

    def zpeer(m):
        return {"blk": flip(b_me, m)}

    def xpeer(d):
        return {"bulk": ((x_me + d) % chips) * 2 + k_me}

    def rcopy(src, dst, ss, rs, where):
        return pltpu.make_async_remote_copy(
            src_ref=src, dst_ref=dst, send_sem=ss, recv_sem=rs, device_id=where, device_id_type=MESH)


    def load_gu(c):
        cols = pl.ds(pl.multiple_of((first_chunk + c) * fc, fc), fc)
        return (pltpu.make_async_copy(wg_hbm.at[:, cols], wg.at[c], g_sem.at[c]),
                pltpu.make_async_copy(wu_hbm.at[:, cols], wu.at[c], u_sem.at[c]))

    def load_d(c):
        rws = pl.ds(pl.multiple_of((first_chunk + c) * fc, fc), fc)
        return pltpu.make_async_copy(wd_hbm.at[rws, :], wd.at[c], d_sem.at[c])


    dims = bits[::-1] + [nb]

    def across_dim(m):
        return across if m == nb else zpeer(m)

    def tok_copy(w, e, m):
        src = (tok_in, cot_in)[w] if e == 0 else got.at[w, e]
        i = dims.index(m)
        return rcopy(src, got.at[w, e + m], tk_send.at[w, e, i], tk_recv.at[w, e + m], across_dim(m))

    def later(e):
        last = max([i for i, m in enumerate(dims) if (e // m) % 2], default=-1)
        return dims[last + 1:]

    def tok_forward(w, e):
        if e:
            rcopy(got.at[w, e], got.at[w, e], tk_send.at[w, e, 0], tk_recv.at[w, e], across).wait_recv()
        for m in later(e):
            tok_copy(w, e, m).start()

    def own_copy(w):
        return pltpu.make_async_copy((tok_in, cot_in)[w], got.at[w, 0], own_sem.at[w])

    def pack(w, scratch, dst):
        for e in range(2 * nb):
            if e >= nb:
                tok_forward(w, e)
            if e == 0:
                own_copy(w).wait()
            scratch[e * rows:(e + 1) * rows, :] = got[w, e].astype(F32)
        dst[...] = scratch[...].astype(BF)


    def js(t):
        return pl.ds(0, 2) if t == 0 else pl.ds(2, 1)

    def pair_copy(t, c):
        return rcopy(part.at[c, 1 - k_me, js(t)], pair.at[c, js(t)], p_send.at[t, c], p_recv.at[t, c], partner)

    def chip_sum(t, c):
        pair_copy(t, c).wait_recv()
        for j in ((0, 1), (2,))[t]:
            chip[c, j] = (part[c, k_me, j] + pair[c, j]).astype(BF)

    def far_copy(t, c, d):
        return rcopy(chip.at[c, js(t)], far.at[c, d - 1, js(t)], f_send.at[t, c, d - 1], f_recv.at[t, c, d - 1],
                     xpeer(d))

    def far_start(t, c):
        for d in range(1, chips):
            far_copy(t, c, d).start()

    def activate(t, c):
        for d in range(1, chips):
            far_copy(t, c, d).wait_recv()

        def total_of(j):
            s = part[c, k_me, j] + pair[c, j]
            for d in range(1, chips):
                s = s + far[c, d - 1, j].astype(F32)
            return s

        if t == 0:
            gate, upward = total_of(0), total_of(1)
            sigma = 1.0 / (1.0 + jnp.exp(-gate))
            live = gate * sigma
            hidden = live * upward
            slope = upward * sigma * (1.0 + gate * (1.0 - sigma))
            if total % n:
                mine = first_chunk + c >= g_me * n
                hidden, live, slope = (jnp.where(mine, v, 0.0) for v in (hidden, live, slope))
            coef[c, 0] = slope
            coef[c, 1] = live
            act[c, k_me, 0] = hidden.astype(BF)
        else:
            back = total_of(2)
            act[c, k_me, 1] = (back * coef[c, 0]).astype(BF)
            act[c, k_me, 2] = (back * coef[c, 1]).astype(BF)

    def ja(t):
        return pl.ds(0, 1) if t == 0 else pl.ds(1, 2)

    def act_copy(t, c):
        return rcopy(act.at[c, k_me, ja(t)], act.at[c, k_me, ja(t)], a_send.at[t, c], a_recv.at[t, c], partner)

    def act_wait(t, c):
        dst = act.at[c, 1 - k_me, ja(t)]
        rcopy(dst, dst, a_send.at[t, c], a_recv.at[t, c], partner).wait_recv()

    def lhs(c, j):
        return jnp.concatenate([act[c, 0, j].astype(F32), act[c, 1, j].astype(F32)], axis=0).astype(BF)


    def acc_of(q):
        acc = mixed if q < PARTS else grad
        return acc, pl.ds((q % PARTS) * pw, pw)

    def y_stage(q):
        acc, cols = acc_of(q)
        ysend[q] = acc[half:, cols].astype(BF)

    def y_copy(q):
        return rcopy(ysend.at[q], yrecv.at[q], y_send.at[q], y_recv.at[q], across)

    def span(s):
        return nb >> (s + 1)

    def z_base(s):
        return nb - (nb >> s)

    def z_copy(q, s):
        blk = pl.ds(z_base(s), span(s))
        return rcopy(zsend.at[q, blk], zrecv.at[q, blk], z_send.at[q, s], z_recv.at[q, s], zpeer(bits[s]))

    def z_stage(q, s):
        acc, cols = acc_of(q)
        if s == 0:
            y_copy(q).wait_recv()
            ysum[q] = acc[:half, cols] + yrecv[q].astype(F32)
        else:
            z_copy(q, s - 1).wait_recv()
            for i in range(span(s - 1)):
                p = i << s
                r = pl.ds(p * rows, rows)
                ysum[q, r, :] = ysum[q, r, :] + zrecv[q, z_base(s - 1) + i].astype(F32)
        if s < steps:
            for i in range(span(s)):
                p = (2 * i + 1) << s
                zsend[q, z_base(s) + i] = ysum[q, p * rows:(p + 1) * rows, :].astype(BF)
        else:
            out[q // PARTS, :, cols] = ysum[q, :rows, :].astype(BF)


    early = min(EARLY, n)
    for c in range(early):
        for cp in load_gu(c):
            cp.start()
    for w in range(2):
        own_copy(w).start()

    barrier = pltpu.get_barrier_semaphore()
    peers = [partner, across] + [zpeer(m) for m in bits] + [xpeer(d) for d in range(1, chips)]
    for where in peers:
        pl.semaphore_signal(barrier, inc=1, device_id=where, device_id_type=MESH)
    pl.semaphore_wait(barrier, len(peers))

    for w in range(2):
        tok_forward(w, 0)
    for c in range(early, n):
        for cp in load_gu(c):
            cp.start()
    for c in range(n):
        load_d(c).start()
    for e in range(1, nb):
        for w in range(2):
            tok_forward(w, e)
    pack(0, mixed, tok)

    def valid(c):
        return jnp.logical_and(c >= 0, c < n)

    def when_valid(c, f):
        pl.when(valid(c))(lambda: f(c))

    two = 2
    groups = pl.cdiv(n, two)

    def members(m):
        return [m * two + i for i in range(two)]

    def each(m, f):
        for c in members(m):
            when_valid(c, f)

    def top(t):
        when_valid(t - 1, lambda c: pair_copy(0, c).start())
        when_valid(t - 4, lambda c: far_start(0, c))

    def bottom(t):
        when_valid(t - 3, lambda c: chip_sum(0, c))

    def keep(c, j, v):
        part[c, 0, j] = v[:half]
        part[c, 1, j] = v[half:]


    def forward(i, _):
        top(i)
        for cp in load_gu(i):
            cp.wait()
        keep(i, 0, jnp.dot(tok[...], wg[i], preferred_element_type=F32))
        keep(i, 1, jnp.dot(tok[...], wu[i], preferred_element_type=F32))
        bottom(i)
        return 0

    lax.fori_loop(0, n, forward, 0)
    pack(1, grad, cot)
    mixed[...] = jnp.zeros_like(mixed)
    grad[...] = jnp.zeros_like(grad)


    def b_top(m):
        each(m - 1, lambda c: pair_copy(1, c).start())
        each(m - 3, lambda c: far_start(1, c))

    def b_bottom(m):
        each(m - 2, lambda c: chip_sum(1, c))

    def grouped(f):
        lax.fori_loop(0, n // two, lambda m, _: f(m, members(m)) or 0, 0)
        if n % two:
            m = jnp.int32(n // two)
            f(m, [c for c in range((n // two) * two, n)])

    def backward(m, cs):
        top(n + m)
        b_top(m)
        activate(0, m)
        for c in cs:
            load_d(c).wait()
        for c in cs:
            keep(c, 2, lax.dot_general(cot[...], wd[c], NT, preferred_element_type=F32))
        act_copy(0, m).start()
        bottom(n + m)
        b_bottom(m)

    grouped(backward)

    def mix(m, cs):
        b_top(groups + m)
        when_valid(groups + m, lambda c: activate(0, c))
        for c in cs:
            act_wait(0, c)
        acc = 0.0
        for c in cs:
            acc = acc + jnp.dot(lhs(c, 0), wd[c], preferred_element_type=F32)
        mixed[...] += acc
        when_valid(groups + m, lambda c: act_copy(0, c).start())
        b_bottom(groups + m)

    grouped(mix)

    ahead = 2
    for g in range(ahead):
        each(jnp.int32(g), lambda c: activate(1, c))
    for q in range(PARTS):
        y_stage(q)
    for g in range(ahead):
        each(jnp.int32(g), lambda c: act_copy(1, c).start())

    def add_grad(lo, hi, cs):
        acc = 0.0
        for c in cs:
            acc = acc + lax.dot_general(lhs(c, 1), wg[c, lo:hi, :], NT, preferred_element_type=F32)
            acc = acc + lax.dot_general(lhs(c, 2), wu[c, lo:hi, :], NT, preferred_element_type=F32)
        grad[:, lo:hi] += acc

    dh = depth // 2

    def grad_a(m, cs):
        @pl.when(m == 0)
        def _():
            for q in range(PARTS):
                y_copy(q).start()

        each(m + ahead, lambda c: activate(1, c))
        for c in cs:
            act_wait(1, c)
        add_grad(0, dh, cs)
        each(m + ahead, lambda c: act_copy(1, c).start())

    grouped(grad_a)

    mh, gh = range(PARTS), range(PARTS, PARTS + PARTS // 2)
    gl = range(PARTS + PARTS // 2, 2 * PARTS)
    for q in gh:
        y_stage(q)
    for q in mh:
        z_stage(q, 0)

    def grad_b(m, cs):
        @pl.when(m == 0)
        def _():
            for q in mh:
                z_copy(q, 0).start()
            for q in gh:
                y_copy(q).start()

        add_grad(dh, depth, cs)

    grouped(grad_b)

    for q in gl:
        y_stage(q)
    for q in mh:
        z_stage(q, 1)
    for q in gl:
        y_copy(q).start()
    for q in gh:
        z_stage(q, 0)
    def z_start(q, s):
        if s < steps:
            z_copy(q, s).start()

    for q in mh:
        z_start(q, 1)
    for q in gh:
        z_start(q, 0)
    for q in gl:
        z_stage(q, 0)
    for q in gl:
        z_start(q, 0)
    for s in range(2, steps + 1):
        for q in mh:
            z_stage(q, s)
        for q in mh:
            z_start(q, s)
    for s in range(1, steps + 1):
        for q in (*gh, *gl):
            z_stage(q, s)
        for q in (*gh, *gl):
            z_start(q, s)


    for w in range(2):
        for e in range(2 * nb):
            for m in later(e):
                tok_copy(w, e, m).wait_send()

    def drain(c, _):
        for t in range(2):
            pair_copy(t, c).wait_send()
            for d in range(1, chips):
                far_copy(t, c, d).wait_send()
            act_copy(t, c).wait_send()
        return 0

    lax.fori_loop(0, n, drain, 0)
    for q in range(2 * PARTS):
        y_copy(q).wait_send()
        for s in range(steps):
            z_copy(q, s).wait_send()


def per_device(ng, nb, nu, tokens, cotangent, gate_weight, up_weight, down_weight):
    rows, depth = tokens.shape
    width = gate_weight.shape[1]
    fc = next(w for w in (256, 128) if width % w == 0)
    total = width // fc
    n = pl.cdiv(total, ng)
    chips = nu // 2
    assert ng == 2 and nb & (nb - 1) == 0 and nb > 1 and nu % 2 == 0 and chips > 1
    assert n >= 7 and depth % (128 * PARTS) == 0 and (rows * nb) % 8 == 0
    half = rows * nb
    t = 2 * half
    pw = depth // PARTS
    steps = nb.bit_length() - 1
    dma = pltpu.SemaphoreType.DMA
    vm = pltpu.VMEM
    both = pl.pallas_call(
        functools.partial(kernel, nb, nu, n, total, fc),
        out_shape=jax.ShapeDtypeStruct((2, rows, depth), BF),
        in_specs=[pl.BlockSpec(memory_space=pl.ANY)] * 5,
        out_specs=pl.BlockSpec(memory_space=pltpu.VMEM),
        scratch_shapes=[
            vm((n, depth, fc), BF), vm((n, depth, fc), BF), vm((n, fc, depth), BF),
            vm((2, 2 * nb, rows, depth), BF), vm((t, depth), BF), vm((t, depth), BF),
            vm((n, 2, 3, half, fc), F32), vm((n, 3, half, fc), F32), vm((n, 3, half, fc), BF),
            vm((n, chips - 1, 3, half, fc), BF), vm((n, 2, half, fc), F32), vm((n, 2, 3, half, fc), BF),
            vm((t, depth), F32), vm((t, depth), F32),
            vm((2 * PARTS, half, pw), BF), vm((2 * PARTS, half, pw), BF), vm((2 * PARTS, half, pw), F32),
            vm((2 * PARTS, nb - 1, rows, pw), BF), vm((2 * PARTS, nb - 1, rows, pw), BF),
            dma((n,)), dma((n,)), dma((n,)), dma((2,)),
            dma((2, 2 * nb, steps + 1)), dma((2, 2 * nb)),
            dma((2, n)), dma((2, n)),
            dma((2, n, chips - 1)), dma((2, n, chips - 1)),
            dma((2, n)), dma((2, n)),
            dma((2 * PARTS,)), dma((2 * PARTS,)),
            dma((2 * PARTS, steps)), dma((2 * PARTS, steps)),
        ],
        compiler_params=pltpu.CompilerParams(
            collective_id=0, has_side_effects=True, vmem_limit_bytes=67043328),
    )(tokens, cotangent, gate_weight, up_weight, down_weight)
    return both[0], both[1]


def solution(mesh):
    return jax.shard_map(
        functools.partial(per_device, mesh.shape["grp"], mesh.shape["blk"], mesh.shape["bulk"]),
        mesh=mesh,
        in_specs=(
            P(("grp", "blk"), "bulk"),
            P(("grp", "blk"), "bulk"),
            P("bulk", "blk"),
            P("bulk", "blk"),
            P("blk", "bulk"),
        ),
        out_specs=(P(("grp", "blk"), "bulk"), P(("grp", "blk"), "bulk")),
        check_vma=False,
    )
```

time: 82.1 us -> 66.9 us (0.81)
  Pallas kernels: 79.7 us -> 64.6 us
  other arithmetic: 0.97 us -> 0 us
  local copies, waits for them, and re-layouts: 0.66 us -> 1.53 us
    pallas_call x1, Pallas kernels: 79.7 us -> 64.6 us  [per_device(): pl.pallas_call(functools.partial(kernel, nb, nu, n, total, fc), out_shape...]
    squeeze x0 -> x1, local copies, waits for them, and re-layouts: none -> 1.53 us  [per_device(): return (both[0], both[1])]
    another operation x1 -> x0, other arithmetic: 0.97 us -> none
where the time goes in v1:
time: 66.9 us; the launch traced here: 66.7 us
  Pallas kernels  64.6 us (97%)
  local copies, waits for them, and re-layouts  1.53 us (2%)
    pallas_call x1, Pallas kernels, per_device(): pl.pallas_call(functools.partial(kernel, nb, nu, n, total, fc), out_shape...  64.6 us
    squeeze x1, local copies, waits for them, and re-layouts, per_device(): return (both[0], both[1])  1.53 us

profile of v1, /device:TPU:0, one launch (start us, length us, event | category | flops | bytes accessed | tf_op | source)
XLA Modules:
  0.0 66.7 jit_solution(13575081871826939852)
XLA Ops:
  0.6 64.6 %shard_map.68 = bf16[2,10,2048]{2,1,0:T(8,128)(2,1)} custom-call(bf16[10,2048]{1,0:T(8,128)(2,1)} %tok_in.1, bf16[10,2048]{1,0:T(8,128)(2,1)} %cot_in.1, bf16[2048,6656]{1,0:T(8,128)(2,1)} %wg_hbm.1, bf16[2048,6656]{1,0:T(8,128)(2,1)} %wu_hbm.1, bf16[6656,2048]{1,0:T(8,128)(2,1)} %wd_hbm.1), custom_call_target="tpu_custom_call" | custom-call | tf_op jit(solution)/shard_map/pallas_call | solution.py:421
  65.2 1.5 %slice_bitcast_fusion = (bf16[10,2048]{1,0:T(8,128)(2,1)}, bf16[10,2048]{1,0:T(8,128)(2,1)}) fusion(bf16[2,10,2048]{2,1,0:T(8,128)(2,1)} %shard_map.68), kind=kLoop, calls=%fused_computation | loop fusion | bytes 163840 | tf_op jit(solution)/shard_map/squeeze | solution.py:445

commit v2 on v1

v2 whole, which is shorter than its diff:
```python
import functools

import jax
import jax.numpy as jnp
from jax import lax
from jax.experimental import pallas as pl
from jax.experimental.pallas import tpu as pltpu
from jax.sharding import PartitionSpec as P

MESH = pl.DeviceIdType.MESH
BF = jnp.bfloat16
F32 = jnp.float32
NT = (((1,), (1,)), ((), ()))
EARLY = 4
PARTS = 4


def flip(i, m):
    return i + m - 2 * m * ((i // m) % 2)


def kernel(nb, nu, n, total, fc, tok_in, cot_in, wg_hbm, wu_hbm, wd_hbm, out,
           wgu, wd, got, tok, cot, part, pair, chip, far, coef, act,
           mixed, grad, ysend, yrecv, ysum, zsend, zrecv,
           gu_sem, d_sem, own_sem, tk_send, tk_recv, p_send, p_recv,
           f_send, f_recv, a_send, a_recv, y_send, y_recv, z_send, z_recv):
    g_me = lax.axis_index("grp")
    b_me = lax.axis_index("blk")
    u_me = lax.axis_index("bulk")
    x_me, k_me = u_me // 2, u_me % 2
    chips = nu // 2
    rows, depth = tok_in.shape
    half = nb * rows
    pw = depth // PARTS
    two, four = 2, 4
    groups = pl.cdiv(n, two)
    steps = nb.bit_length() - 1
    bits = [1 << s for s in range(steps)]
    first_chunk = jnp.minimum(g_me * n, total - n)
    partner = {"bulk": x_me * 2 + (1 - k_me)}
    across = {"grp": 1 - g_me}

    def zpeer(m):
        return {"blk": flip(b_me, m)}

    def xpeer(d):
        return {"bulk": ((x_me + d) % chips) * 2 + k_me}

    def rcopy(src, dst, ss, rs, where):
        return pltpu.make_async_remote_copy(
            src_ref=src, dst_ref=dst, send_sem=ss, recv_sem=rs, device_id=where, device_id_type=MESH)


    def load_gu(c):
        cols = pl.ds(pl.multiple_of((first_chunk + c) * fc, fc), fc)
        return (pltpu.make_async_copy(wg_hbm.at[:, cols], wgu.at[c, 0], gu_sem.at[c]),
                pltpu.make_async_copy(wu_hbm.at[:, cols], wgu.at[c, 1], gu_sem.at[c]))

    def wait_gu(c):
        pltpu.make_async_copy(wgu.at[c], wgu.at[c], gu_sem.at[c]).wait()

    def load_d(m, c, cnt):
        src = pl.ds(pl.multiple_of((first_chunk + c) * fc, fc), cnt * fc)
        dst = pl.ds(pl.multiple_of(c * fc, fc), cnt * fc)
        return pltpu.make_async_copy(wd_hbm.at[src, :], wd.at[dst, :], d_sem.at[m])

    def wd_of(c):
        return wd[pl.ds(pl.multiple_of(c * fc, fc), fc), :]


    dims = bits[::-1] + [nb]

    def across_dim(m):
        return across if m == nb else zpeer(m)

    def tok_copy(w, e, m):
        return rcopy(got.at[w, e], got.at[w, e + m], tk_send.at[w], tk_recv.at[w, e + m], across_dim(m))

    def later(e):
        last = max([i for i, m in enumerate(dims) if (e // m) % 2], default=-1)
        return dims[last + 1:]

    def tok_forward(w, e):
        if e:
            rcopy(got.at[w, e], got.at[w, e], tk_send.at[w], tk_recv.at[w, e], across).wait_recv()
        for m in later(e):
            tok_copy(w, e, m).start()

    def own_copy(w):
        return pltpu.make_async_copy((tok_in, cot_in)[w], got.at[w, 0], own_sem.at[w])

    def pack(w, scratch, dst):
        for e in range(2 * nb):
            if e >= nb:
                tok_forward(w, e)
            scratch[e * rows:(e + 1) * rows, :] = got[w, e].astype(F32)
        dst[...] = scratch[...].astype(BF)


    def js(t):
        return pl.ds(0, 2) if t == 0 else pl.ds(2, 1)

    def rows_of(t, m, cnt):
        return pl.ds(m if t == 0 else m * two, cnt)

    def pair_copy(t, m, cnt):
        r = rows_of(t, m, cnt)
        return rcopy(part.at[r, 1 - k_me, js(t)], pair.at[r, js(t)], p_send.at[t], p_recv.at[t, m], partner)

    def chip_sum(t, m, cnt):
        pair_copy(t, m, cnt).wait_recv()
        for i in range(cnt):
            c = m if t == 0 else m * two + i
            for j in ((0, 1), (2,))[t]:
                chip[c, j] = (part[c, k_me, j] + pair[c, j]).astype(BF)

    def far_copy(t, m, cnt, d):
        r = rows_of(t, m, cnt)
        return rcopy(chip.at[r, js(t)], far.at[d - 1, r, js(t)], f_send.at[t, d - 1], f_recv.at[t, m, d - 1],
                     xpeer(d))

    def far_start(t, m, cnt):
        for d in range(1, chips):
            far_copy(t, m, cnt, d).start()

    def activate(t, m, cnt):
        for d in range(1, chips):
            far_copy(t, m, cnt, d).wait_recv()
        for i in range(cnt):
            values(t, m if t == 0 else m * two + i)

    def values(t, c):
        def total_of(j):
            s = part[c, k_me, j] + pair[c, j]
            for d in range(1, chips):
                s = s + far[d - 1, c, j].astype(F32)
            return s

        if t == 0:
            gate, upward = total_of(0), total_of(1)
            sigma = 1.0 / (1.0 + jnp.exp(-gate))
            live = gate * sigma
            hidden = live * upward
            slope = upward * sigma * (1.0 + gate * (1.0 - sigma))
            if total % n:
                mine = first_chunk + c >= g_me * n
                hidden, live, slope = (jnp.where(mine, v, 0.0) for v in (hidden, live, slope))
            coef[c, 0] = slope
            coef[c, 1] = live
            act[c, k_me, 0] = hidden.astype(BF)
        else:
            back = total_of(2)
            act[c, k_me, 1] = (back * coef[c, 0]).astype(BF)
            act[c, k_me, 2] = (back * coef[c, 1]).astype(BF)

    def ja(t):
        return pl.ds(0, 1) if t == 0 else pl.ds(1, 2)

    def act_copy(t, m, cnt):
        r = rows_of(t, m, cnt)
        ref = act.at[r, k_me, ja(t)]
        return rcopy(ref, ref, a_send.at[t], a_recv.at[t, m], partner)

    def act_wait(t, m, cnt):
        ref = act.at[rows_of(t, m, cnt), 1 - k_me, ja(t)]
        rcopy(ref, ref, a_send.at[t], a_recv.at[t, m], partner).wait_recv()

    def lhs(c, j):
        return jnp.concatenate([act[c, 0, j].astype(F32), act[c, 1, j].astype(F32)], axis=0).astype(BF)


    outs = [(0, PARTS), (PARTS, 2), (PARTS + 2, 1), (PARTS + 3, 1)]

    def acc_of(q):
        acc = mixed if q < PARTS else grad
        return acc, pl.ds((q % PARTS) * pw, pw)

    def run(o):
        return range(outs[o][0], sum(outs[o]))

    def y_stage(o):
        for q in run(o):
            acc, cols = acc_of(q)
            ysend[q] = acc[half:, cols].astype(BF)

    def y_copy(o):
        qs = pl.ds(*outs[o])
        return rcopy(ysend.at[qs], yrecv.at[qs], y_send.at[0], y_recv.at[o], across)

    def span(s):
        return nb >> (s + 1)

    def z_base(s):
        return nb - (nb >> s)

    def z_copy(o, s):
        at = (pl.ds(*outs[o]), pl.ds(z_base(s), span(s)))
        return rcopy(zsend.at[at], zrecv.at[at], z_send.at[s], z_recv.at[o, s], zpeer(bits[s]))

    def z_stage(o, s):
        (y_copy(o) if s == 0 else z_copy(o, s - 1)).wait_recv()
        for q in run(o):
            acc, cols = acc_of(q)
            if s == 0:
                ysum[q] = acc[:half, cols] + yrecv[q].astype(F32)
            else:
                for i in range(span(s - 1)):
                    p = i << s
                    r = pl.ds(p * rows, rows)
                    ysum[q, r, :] = ysum[q, r, :] + zrecv[q, z_base(s - 1) + i].astype(F32)
            if s < steps:
                for i in range(span(s)):
                    p = (2 * i + 1) << s
                    zsend[q, z_base(s) + i] = ysum[q, p * rows:(p + 1) * rows, :].astype(BF)
            else:
                out[q // PARTS, :, cols] = ysum[q, :rows, :].astype(BF)

    def z_start(o, s):
        if s < steps:
            z_copy(o, s).start()

    def z_step(o, s):
        if s <= steps:
            z_stage(o, s)
            z_start(o, s)


    def valid(c):
        return jnp.logical_and(c >= 0, c < n)

    def chunk(c, f):
        pl.when(valid(c))(lambda: f(c, 1))

    def group(m, f):
        pl.when(jnp.logical_and(m >= 0, m < n // two))(lambda: f(m, two))
        if n % two:
            pl.when(m == n // two)(lambda: f(n // two, n % two))

    def grouped(size, f):
        lax.fori_loop(0, n // size, lambda m, _: f(m, [m * size + i for i in range(size)]) or 0, 0)
        if n % size:
            f(jnp.int32(n // size), list(range(n - n % size, n)))

    def at(m, size, k, f):
        pl.when(m == min(k, pl.cdiv(n, size) - 1))(f)


    early = min(EARLY, n)
    own_copy(0).start()
    own_copy(1).start()
    for c in range(early):
        for cp in load_gu(c):
            cp.start()

    barrier = pltpu.get_barrier_semaphore()
    peers = [partner, across] + [zpeer(m) for m in bits] + [xpeer(d) for d in range(1, chips)]
    for where in peers:
        pl.semaphore_signal(barrier, inc=1, device_id=where, device_id_type=MESH)
    own_copy(0).wait()
    own_copy(1).wait()
    pl.semaphore_wait(barrier, len(peers))

    tok_forward(0, 0)
    for c in range(early, n):
        for cp in load_gu(c):
            cp.start()
    for m in range(groups):
        load_d(m, m * two, min(two, n - m * two)).start()
    for e in range(1, nb):
        tok_forward(0, e)
    tok_forward(1, 0)
    pack(0, mixed, tok)

    def top(t):
        chunk(t - 1, lambda c, i: pair_copy(0, c, i).start())
        chunk(t - 4, lambda c, i: far_start(0, c, i))

    def bottom(t):
        chunk(t - 3, lambda c, i: chip_sum(0, c, i))

    def keep(c, j, v):
        part[c, 0, j] = v[:half]
        part[c, 1, j] = v[half:]


    def forward(i, _):
        top(i)
        for e in range(1, nb):
            at(i, 1, 4 + (6 * (e - 1)) // (nb - 1), lambda e=e: tok_forward(1, e))
        wait_gu(i)
        keep(i, 0, jnp.dot(tok[...], wgu[i, 0], preferred_element_type=F32))
        keep(i, 1, jnp.dot(tok[...], wgu[i, 1], preferred_element_type=F32))
        bottom(i)
        return 0

    lax.fori_loop(0, n, forward, 0)
    pack(1, grad, cot)
    mixed[...] = jnp.zeros_like(mixed)
    grad[...] = jnp.zeros_like(grad)


    def b_top(m):
        group(m - 1, lambda g, i: pair_copy(1, g, i).start())
        group(m - 3, lambda g, i: far_start(1, g, i))

    def b_bottom(m):
        group(m - 2, lambda g, i: chip_sum(1, g, i))

    def backward(m, cs):
        top(n + m)
        b_top(m)
        activate(0, m, 1)
        load_d(m, cs[0], len(cs)).wait()
        for c in cs:
            keep(c, 2, lax.dot_general(cot[...], wd_of(c), NT, preferred_element_type=F32))
        act_copy(0, m, 1).start()
        bottom(n + m)
        b_bottom(m)

    grouped(two, backward)

    def mix(m, cs):
        b_top(groups + m)
        chunk(groups + m, lambda c, i: activate(0, c, i))
        for c in cs:
            act_wait(0, c, 1)
        acc = 0.0
        for c in cs:
            acc = acc + jnp.dot(lhs(c, 0), wd_of(c), preferred_element_type=F32)
        mixed[...] += acc
        chunk(groups + m, lambda c, i: act_copy(0, c, i).start())
        b_bottom(groups + m)

    grouped(two, mix)

    def add_grad(lo, hi, cs):
        acc = 0.0
        for c in cs:
            acc = acc + lax.dot_general(lhs(c, 1), wgu[c, 0, lo:hi, :], NT, preferred_element_type=F32)
            acc = acc + lax.dot_general(lhs(c, 2), wgu[c, 1, lo:hi, :], NT, preferred_element_type=F32)
        grad[:, lo:hi] += acc

    ahead = 2
    for g in range(ahead):
        activate(1, g, two)
    y_stage(0)
    for g in range(ahead):
        act_copy(1, g, two).start()

    def grad_a(m, cs):
        at(m, two, 0, lambda: y_copy(0).start())
        at(m, two, 5, lambda: z_stage(0, 0))
        at(m, two, 6, lambda: z_start(0, 0))
        group(m + ahead, lambda g, i: activate(1, g, i))
        act_wait(1, m, len(cs))
        add_grad(0, 2 * pw, cs)
        group(m + ahead, lambda g, i: act_copy(1, g, i).start())

    grouped(two, grad_a)
    y_stage(1)

    def grad_b(m, cs):
        at(m, four, 0, lambda: y_copy(1).start())
        at(m, four, 2, lambda: z_stage(0, 1))
        at(m, four, 3, lambda: z_start(0, 1))
        add_grad(2 * pw, 3 * pw, cs)

    grouped(four, grad_b)
    y_stage(2)

    def grad_c(m, cs):
        at(m, four, 0, lambda: y_copy(2).start())
        at(m, four, 1, lambda: z_stage(1, 0))
        at(m, four, 2, lambda: z_start(1, 0))
        add_grad(3 * pw, depth, cs)

    grouped(four, grad_c)
    y_stage(3)
    y_copy(3).start()
    z_step(2, 0)
    z_step(1, 1)
    z_step(0, 2)
    z_step(2, 1)
    z_step(3, 0)
    z_step(1, 2)
    z_step(3, 1)
    z_step(2, 2)
    z_step(3, 2)
    for s in range(3, steps + 1):
        for o in range(len(outs)):
            z_step(o, s)


    def left(ref, sem):
        rcopy(ref, ref, sem, sem, across).wait_send()

    for w in range(2):
        left(got.at[w, pl.ds(1, 2 * nb - 1)], tk_send.at[w])
    for t in range(2):
        left(part.at[:, 0, js(t)], p_send.at[t])
        for d in range(1, chips):
            left(chip.at[:, js(t)], f_send.at[t, d - 1])
        left(act.at[:, 0, ja(t)], a_send.at[t])
    left(ysend, y_send.at[0])
    for s in range(steps):
        left(zsend.at[:, pl.ds(z_base(s), span(s))], z_send.at[s])


def per_device(ng, nb, nu, tokens, cotangent, gate_weight, up_weight, down_weight):
    rows, depth = tokens.shape
    width = gate_weight.shape[1]
    fc = next(w for w in (256, 128) if width % w == 0)
    total = width // fc
    n = pl.cdiv(total, ng)
    chips = nu // 2
    assert ng == 2 and nb & (nb - 1) == 0 and nb > 1 and nu % 2 == 0 and chips > 1
    assert n >= 7 and depth % (128 * PARTS) == 0 and (rows * nb) % 8 == 0
    half = rows * nb
    t = 2 * half
    pw = depth // PARTS
    steps = nb.bit_length() - 1
    dma = pltpu.SemaphoreType.DMA
    vm = pltpu.VMEM
    both = pl.pallas_call(
        functools.partial(kernel, nb, nu, n, total, fc),
        out_shape=vm((2, rows, depth), BF),
        in_specs=[pl.BlockSpec(memory_space=pl.ANY)] * 5,
        out_specs=pl.BlockSpec(memory_space=pltpu.VMEM),
        scratch_shapes=[
            vm((n, 2, depth, fc), BF), vm((n * fc, depth), BF),
            vm((2, 2 * nb, rows, depth), BF), vm((t, depth), BF), vm((t, depth), BF),
            vm((n, 2, 3, half, fc), F32), vm((n, 3, half, fc), F32), vm((n, 3, half, fc), BF),
            vm((chips - 1, n, 3, half, fc), BF), vm((n, 2, half, fc), F32), vm((n, 2, 3, half, fc), BF),
            vm((t, depth), F32), vm((t, depth), F32),
            vm((2 * PARTS, half, pw), BF), vm((2 * PARTS, half, pw), BF), vm((2 * PARTS, half, pw), F32),
            vm((2 * PARTS, nb - 1, rows, pw), BF), vm((2 * PARTS, nb - 1, rows, pw), BF),
            dma((n,)), dma((pl.cdiv(n, 2),)), dma((2,)), dma((2,)), dma((2, 2 * nb)),
            dma((2,)), dma((2, n)), dma((2, chips - 1)), dma((2, n, chips - 1)), dma((2,)), dma((2, n)),
            dma((1,)), dma((PARTS,)), dma((steps,)), dma((PARTS, steps)),
        ],
        compiler_params=pltpu.CompilerParams(
            collective_id=0, has_side_effects=True, vmem_limit_bytes=67043328 - 4 * depth * pl.cdiv(rows, 16) * 16),
    )(tokens, cotangent, gate_weight, up_weight, down_weight)
    return both[0], both[1]


def solution(mesh):
    return jax.shard_map(
        functools.partial(per_device, mesh.shape["grp"], mesh.shape["blk"], mesh.shape["bulk"]),
        mesh=mesh,
        in_specs=(
            P(("grp", "blk"), "bulk"),
            P(("grp", "blk"), "bulk"),
            P("bulk", "blk"),
            P("bulk", "blk"),
            P("blk", "bulk"),
        ),
        out_specs=(P(("grp", "blk"), "bulk"), P(("grp", "blk"), "bulk")),
        check_vma=False,
    )
```

time: 66.9 us -> 67.4 us (level)
  Pallas kernels: 64.6 us -> 65.9 us
  local copies, waits for them, and re-layouts: 1.53 us -> 0.66 us
    pallas_call x1, Pallas kernels: 64.6 us -> 65.9 us  [per_device(): pl.pallas_call(functools.partial(kernel, nb, nu, n, total, fc), out_shape...]
    squeeze x1, local copies, waits for them, and re-layouts: 1.53 us -> 0.66 us  [per_device(): return (both[0], both[1])]
where the time goes in v2:
time: 67.4 us; the launch traced here: 67.2 us
  Pallas kernels  65.9 us (98%)
    pallas_call x1, Pallas kernels, per_device(): pl.pallas_call(functools.partial(kernel, nb, nu, n, total, fc), out_shape...  65.9 us

profile of v2, /device:TPU:0, one launch (start us, length us, event | category | flops | bytes accessed | tf_op | source)
XLA Modules:
  0.0 67.2 jit_solution(3676040105531586173)
XLA Ops:
  0.6 65.9 %shard_map.68 = bf16[2,10,2048]{2,1,0:T(8,128)(2,1)S(1)} custom-call(bf16[10,2048]{1,0:T(8,128)(2,1)} %tok_in.1, bf16[10,2048]{1,0:T(8,128)(2,1)} %cot_in.1, bf16[2048,6656]{1,0:T(8,128)(2,1)} %wg_hbm.1, bf16[2048,6656]{1,0:T(8,128)(2,1)} %wu_hbm.1, bf16[6656,2048]{1,0:T(8,128)(2,1)} %wd_hbm.1), custom_call_target="tpu_custom_call" | custom-call | tf_op jit(solution)/shard_map/pallas_call | solution.py:424
  66.6 0.7 slice_bitcast_fusion

commit v3 on v2

--- a/solution.py
+++ b/solution.py
@@ -11,7 +11,6 @@
 BF = jnp.bfloat16
 F32 = jnp.float32
 NT = (((1,), (1,)), ((), ()))
-EARLY = 4
 PARTS = 4
 
 
@@ -20,7 +19,7 @@
 
 
 def kernel(nb, nu, n, total, fc, tok_in, cot_in, wg_hbm, wu_hbm, wd_hbm, out,
-           wgu, wd, got, tok, cot, part, pair, chip, far, coef, act,
+           wgu, wd, own, folded, got, tok, cot, part, pair, chip, far, coef, act,
            mixed, grad, ysend, yrecv, ysum, zsend, zrecv,
            gu_sem, d_sem, own_sem, tk_send, tk_recv, p_send, p_recv,
            f_send, f_recv, a_send, a_recv, y_send, y_recv, z_send, z_recv):
@@ -69,31 +68,57 @@
 
 
     dims = bits[::-1] + [nb]
+    fold, wide = got.shape[3] // rows, got.shape[4]
 
     def across_dim(m):
         return across if m == nb else zpeer(m)
 
-    def tok_copy(w, e, m):
-        return rcopy(got.at[w, e], got.at[w, e + m], tk_send.at[w], tk_recv.at[w, e + m], across_dim(m))
+    def tok_ref(w, e, h):
+        return got.at[w, e, h]
+
+    def tok_copy(w, e, m, h):
+        return rcopy(tok_ref(w, e, h), tok_ref(w, e + m, h), tk_send.at[w], tk_recv.at[w, e + m, h], across_dim(m))
+
+    def tok_wait(w, e, h):
+        rcopy(tok_ref(w, e, h), tok_ref(w, e, h), tk_send.at[w], tk_recv.at[w, e, h], across).wait_recv()
 
     def later(e):
         last = max([i for i, m in enumerate(dims) if (e // m) % 2], default=-1)
         return dims[last + 1:]
 
     def tok_forward(w, e):
-        if e:
-            rcopy(got.at[w, e], got.at[w, e], tk_send.at[w], tk_recv.at[w, e], across).wait_recv()
-        for m in later(e):
-            tok_copy(w, e, m).start()
+        if e == 0:
+            for m in later(e):
+                for h in range(2):
+                    tok_copy(w, e, m, h).start()
+        else:
+            for h in range(2):
+                tok_wait(w, e, h)
+                for m in later(e):
+                    tok_copy(w, e, m, h).start()
 
     def own_copy(w):
-        return pltpu.make_async_copy((tok_in, cot_in)[w], got.at[w, 0], own_sem.at[w])
+        return pltpu.make_async_copy((tok_in, cot_in)[w], own.at[w], own_sem.at[w])
+
+    def place(h, j):
+        lo = (h * fold + j) * wide
+        return slice(lo, lo + wide)
+
+    def fold_own(w):
+        own_copy(w).wait()
+        for h in range(2):
+            for j in range(fold):
+                folded[w, h, j * rows:(j + 1) * rows, :] = own[w, :, place(h, j)].astype(F32)
+        got[w, 0] = folded[w].astype(BF)
 
     def pack(w, scratch, dst):
         for e in range(2 * nb):
-            if e >= nb:
-                tok_forward(w, e)
-            scratch[e * rows:(e + 1) * rows, :] = got[w, e].astype(F32)
+            for h in range(2):
+                if e >= nb:
+                    tok_wait(w, e, h)
+                for j in range(fold):
+                    scratch[e * rows:(e + 1) * rows, place(h, j)] = (
+                        got[w, e, h, j * rows:(j + 1) * rows, :].astype(F32))
         dst[...] = scratch[...].astype(BF)
 
 
@@ -245,30 +270,27 @@
         pl.when(m == min(k, pl.cdiv(n, size) - 1))(f)
 
 
-    early = min(EARLY, n)
-    own_copy(0).start()
-    own_copy(1).start()
-    for c in range(early):
-        for cp in load_gu(c):
-            cp.start()
-
     barrier = pltpu.get_barrier_semaphore()
     peers = [partner, across] + [zpeer(m) for m in bits] + [xpeer(d) for d in range(1, chips)]
     for where in peers:
         pl.semaphore_signal(barrier, inc=1, device_id=where, device_id_type=MESH)
-    own_copy(0).wait()
-    own_copy(1).wait()
-    pl.semaphore_wait(barrier, len(peers))
-
-    tok_forward(0, 0)
-    for c in range(early, n):
+    for w in range(2):
+        own_copy(w).start()
+    for w in range(2):
+        fold_own(w)
+    for c in range(n):
         for cp in load_gu(c):
             cp.start()
     for m in range(groups):
         load_d(m, m * two, min(two, n - m * two)).start()
+    pl.semaphore_wait(barrier, len(peers))
+
+    for w in range(2):
+        tok_forward(w, 0)
     for e in range(1, nb):
         tok_forward(0, e)
-    tok_forward(1, 0)
+    for e in range(1, nb - 1):
+        tok_forward(1, e)
     pack(0, mixed, tok)
 
     def top(t):
@@ -285,8 +307,7 @@
 
     def forward(i, _):
         top(i)
-        for e in range(1, nb):
-            at(i, 1, 4 + (6 * (e - 1)) // (nb - 1), lambda e=e: tok_forward(1, e))
+        at(i, 1, 3, lambda: tok_forward(1, nb - 1))
         wait_gu(i)
         keep(i, 0, jnp.dot(tok[...], wgu[i, 0], preferred_element_type=F32))
         keep(i, 1, jnp.dot(tok[...], wgu[i, 1], preferred_element_type=F32))
@@ -419,6 +440,8 @@
     t = 2 * half
     pw = depth // PARTS
     steps = nb.bit_length() - 1
+    fold = next((f for f in (1, 2, 4, 8) if rows * f % 8 == 0 and depth % (256 * f) == 0), 1)
+    wide = depth // (2 * fold)
     dma = pltpu.SemaphoreType.DMA
     vm = pltpu.VMEM
     both = pl.pallas_call(
@@ -428,13 +451,14 @@
         out_specs=pl.BlockSpec(memory_space=pltpu.VMEM),
         scratch_shapes=[
             vm((n, 2, depth, fc), BF), vm((n * fc, depth), BF),
-            vm((2, 2 * nb, rows, depth), BF), vm((t, depth), BF), vm((t, depth), BF),
+            vm((2, rows, depth), BF), vm((2, 2, rows * fold, wide), F32),
+            vm((2, 2 * nb, 2, rows * fold, wide), BF), vm((t, depth), BF), vm((t, depth), BF),
             vm((n, 2, 3, half, fc), F32), vm((n, 3, half, fc), F32), vm((n, 3, half, fc), BF),
             vm((chips - 1, n, 3, half, fc), BF), vm((n, 2, half, fc), F32), vm((n, 2, 3, half, fc), BF),
             vm((t, depth), F32), vm((t, depth), F32),
             vm((2 * PARTS, half, pw), BF), vm((2 * PARTS, half, pw), BF), vm((2 * PARTS, half, pw), F32),
             vm((2 * PARTS, nb - 1, rows, pw), BF), vm((2 * PARTS, nb - 1, rows, pw), BF),
-            dma((n,)), dma((pl.cdiv(n, 2),)), dma((2,)), dma((2,)), dma((2, 2 * nb)),
+            dma((n,)), dma((pl.cdiv(n, 2),)), dma((2,)), dma((2,)), dma((2, 2 * nb, 2)),
             dma((2,)), dma((2, n)), dma((2, chips - 1)), dma((2, n, chips - 1)), dma((2,)), dma((2, n)),
             dma((1,)), dma((PARTS,)), dma((steps,)), dma((PARTS, steps)),
         ],

time: 67.4 us -> 61.1 us (0.907)
  Pallas kernels: 65.9 us -> 59.6 us
    pallas_call x1, Pallas kernels: 65.9 us -> 59.6 us  [per_device(): pl.pallas_call(functools.partial(kernel, nb, nu, n, total, fc), out_shape...]
where the time goes in v3:
time: 61.1 us; the launch traced here: 60.9 us
  Pallas kernels  59.6 us (98%)
  local copies, waits for them, and re-layouts  0.66 us (1%)
  between operations  0.64 us (1%)
    pallas_call x1, Pallas kernels, per_device(): pl.pallas_call(functools.partial(kernel, nb, nu, n, total, fc), out_shape...  59.6 us

profile of v3, /device:TPU:0, one launch (start us, length us, event | category | flops | bytes accessed | tf_op | source)
XLA Modules:
  0.0 60.9 jit_solution(17866391736875085916)
XLA Ops:
  0.6 59.6 %shard_map.68 = bf16[2,10,2048]{2,1,0:T(8,128)(2,1)S(1)} custom-call(bf16[10,2048]{1,0:T(8,128)(2,1)} %tok_in.1, bf16[10,2048]{1,0:T(8,128)(2,1)} %cot_in.1, bf16[2048,6656]{1,0:T(8,128)(2,1)} %wg_hbm.1, bf16[2048,6656]{1,0:T(8,128)(2,1)} %wu_hbm.1, bf16[6656,2048]{1,0:T(8,128)(2,1)} %wd_hbm.1), custom_call_target="tpu_custom_call" | custom-call | tf_op jit(solution)/shard_map/pallas_call | solution.py:447
  60.3 0.7 %slice_bitcast_fusion = (bf16[10,2048]{1,0:T(8,128)(2,1)}, bf16[10,2048]{1,0:T(8,128)(2,1)}) fusion(bf16[2,10,2048]{2,1,0:T(8,128)(2,1)S(1)} %shard_map.68), kind=kLoop, calls=%fused_computation | loop fusion | bytes 163840 | tf_op jit(solution)/shard_map/squeeze | solution.py:468

commit v4 on v3

--- a/solution.py
+++ b/solution.py
@@ -12,17 +12,25 @@
 F32 = jnp.float32
 NT = (((1,), (1,)), ((), ()))
 PARTS = 4
+SIZE = 4
 
 
 def flip(i, m):
     return i + m - 2 * m * ((i // m) % 2)
 
 
+def flips(i, bits):
+    for s in range(bits.bit_length()):
+        if bits >> s & 1:
+            i = flip(i, 1 << s)
+    return i
+
+
 def kernel(nb, nu, n, total, fc, tok_in, cot_in, wg_hbm, wu_hbm, wd_hbm, out,
            wgu, wd, own, folded, got, tok, cot, part, pair, chip, far, coef, act,
-           mixed, grad, ysend, yrecv, ysum, zsend, zrecv,
+           mixed, grad, ysend, yrecv, ysum, zflat, zsend, zrecv, lflat, lsend, lrecv,
            gu_sem, d_sem, own_sem, tk_send, tk_recv, p_send, p_recv,
-           f_send, f_recv, a_send, a_recv, y_send, y_recv, z_send, z_recv):
+           f_send, f_recv, a_send, a_recv, y_send, y_recv, z_send, z_recv, l_send, l_recv):
     g_me = lax.axis_index("grp")
     b_me = lax.axis_index("blk")
     u_me = lax.axis_index("bulk")
@@ -31,8 +39,8 @@
     rows, depth = tok_in.shape
     half = nb * rows
     pw = depth // PARTS
-    two, four = 2, 4
-    groups = pl.cdiv(n, two)
+    size = SIZE
+    groups = pl.cdiv(n, size)
     steps = nb.bit_length() - 1
     bits = [1 << s for s in range(steps)]
     first_chunk = jnp.minimum(g_me * n, total - n)
@@ -69,6 +77,7 @@
 
     dims = bits[::-1] + [nb]
     fold, wide = got.shape[3] // rows, got.shape[4]
+    zfold, zwide = zsend.shape[2] // rows, zsend.shape[3]
 
     def across_dim(m):
         return across if m == nb else zpeer(m)
@@ -126,7 +135,7 @@
         return pl.ds(0, 2) if t == 0 else pl.ds(2, 1)
 
     def rows_of(t, m, cnt):
-        return pl.ds(m if t == 0 else m * two, cnt)
+        return pl.ds(m if t == 0 else m * size, cnt)
 
     def pair_copy(t, m, cnt):
         r = rows_of(t, m, cnt)
@@ -135,7 +144,7 @@
     def chip_sum(t, m, cnt):
         pair_copy(t, m, cnt).wait_recv()
         for i in range(cnt):
-            c = m if t == 0 else m * two + i
+            c = m if t == 0 else m * size + i
             for j in ((0, 1), (2,))[t]:
                 chip[c, j] = (part[c, k_me, j] + pair[c, j]).astype(BF)
 
@@ -152,7 +161,7 @@
         for d in range(1, chips):
             far_copy(t, m, cnt, d).wait_recv()
         for i in range(cnt):
-            values(t, m if t == 0 else m * two + i)
+            values(t, m if t == 0 else m * size + i)
 
     def values(t, c):
         def total_of(j):
@@ -194,7 +203,7 @@
         return jnp.concatenate([act[c, 0, j].astype(F32), act[c, 1, j].astype(F32)], axis=0).astype(BF)
 
 
-    outs = [(0, PARTS), (PARTS, 2), (PARTS + 2, 1), (PARTS + 3, 1)]
+    outs = [(0, PARTS), (PARTS, 2), (PARTS + 2, 1)]
 
     def acc_of(q):
         acc = mixed if q < PARTS else grad
@@ -232,11 +241,17 @@
                 for i in range(span(s - 1)):
                     p = i << s
                     r = pl.ds(p * rows, rows)
-                    ysum[q, r, :] = ysum[q, r, :] + zrecv[q, z_base(s - 1) + i].astype(F32)
+                    for j in range(zfold):
+                        cs = pl.ds(j * zwide, zwide)
+                        ysum[q, r, cs] = ysum[q, r, cs] + (
+                            zrecv[q, z_base(s - 1) + i, j * rows:(j + 1) * rows, :].astype(F32))
             if s < steps:
                 for i in range(span(s)):
                     p = (2 * i + 1) << s
-                    zsend[q, z_base(s) + i] = ysum[q, p * rows:(p + 1) * rows, :].astype(BF)
+                    for j in range(zfold):
+                        zflat[q, i, j * rows:(j + 1) * rows, :] = (
+                            ysum[q, p * rows:(p + 1) * rows, j * zwide:(j + 1) * zwide])
+                    zsend[q, z_base(s) + i] = zflat[q, i].astype(BF)
             else:
                 out[q // PARTS, :, cols] = ysum[q, :rows, :].astype(BF)
 
@@ -250,6 +265,30 @@
             z_start(o, s)
 
 
+    def last_peer(e):
+        return {"grp": flip(g_me, 1) if e >= nb else g_me, "blk": flips(b_me, e % nb)}
+
+    def last_stage():
+        for e in range(1, 2 * nb):
+            for j in range(zfold):
+                lflat[e - 1, j * rows:(j + 1) * rows, :] = (
+                    grad[e * rows:(e + 1) * rows, depth - pw + j * zwide:depth - pw + (j + 1) * zwide])
+        lsend[...] = lflat[...].astype(BF)
+
+    def last_copy(e):
+        return rcopy(lsend.at[e - 1], lrecv.at[e - 1], l_send.at[0], l_recv.at[e - 1], last_peer(e))
+
+    def last_sum():
+        for e in range(1, 2 * nb):
+            last_copy(e).wait_recv()
+        for j in range(zfold):
+            lo = depth - pw + j * zwide
+            v = grad[:rows, lo:lo + zwide]
+            for e in range(1, 2 * nb):
+                v = v + lrecv[e - 1, j * rows:(j + 1) * rows, :].astype(F32)
+            out[1, :, lo:lo + zwide] = v.astype(BF)
+
+
     def valid(c):
         return jnp.logical_and(c >= 0, c < n)
 
@@ -257,17 +296,17 @@
         pl.when(valid(c))(lambda: f(c, 1))
 
     def group(m, f):
-        pl.when(jnp.logical_and(m >= 0, m < n // two))(lambda: f(m, two))
-        if n % two:
-            pl.when(m == n // two)(lambda: f(n // two, n % two))
-
-    def grouped(size, f):
+        pl.when(jnp.logical_and(m >= 0, m < n // size))(lambda: f(m, size))
+        if n % size:
+            pl.when(m == n // size)(lambda: f(n // size, n % size))
+
+    def grouped(f):
         lax.fori_loop(0, n // size, lambda m, _: f(m, [m * size + i for i in range(size)]) or 0, 0)
         if n % size:
             f(jnp.int32(n // size), list(range(n - n % size, n)))
 
-    def at(m, size, k, f):
-        pl.when(m == min(k, pl.cdiv(n, size) - 1))(f)
+    def at(m, k, f):
+        pl.when(m == min(k, groups - 1))(f)
 
 
     barrier = pltpu.get_barrier_semaphore()
@@ -282,7 +321,7 @@
         for cp in load_gu(c):
             cp.start()
     for m in range(groups):
-        load_d(m, m * two, min(two, n - m * two)).start()
+        load_d(m, m * size, min(size, n - m * size)).start()
     pl.semaphore_wait(barrier, len(peers))
 
     for w in range(2):
@@ -295,22 +334,30 @@
 
     def top(t):
         chunk(t - 1, lambda c, i: pair_copy(0, c, i).start())
-        chunk(t - 4, lambda c, i: far_start(0, c, i))
+        chunk(t - 3, lambda c, i: far_start(0, c, i))
 
     def bottom(t):
-        chunk(t - 3, lambda c, i: chip_sum(0, c, i))
+        chunk(t - 2, lambda c, i: chip_sum(0, c, i))
 
     def keep(c, j, v):
         part[c, 0, j] = v[:half]
         part[c, 1, j] = v[half:]
 
 
+    soon = max(0, n - 10)
+
     def forward(i, _):
         top(i)
-        at(i, 1, 3, lambda: tok_forward(1, nb - 1))
+        chunk(i - n + soon, lambda c, _: activate(0, c, 1))
+
+        @pl.when(i == min(7, n - 1))
+        def _():
+            tok_forward(1, nb - 1)
+
         wait_gu(i)
         keep(i, 0, jnp.dot(tok[...], wgu[i, 0], preferred_element_type=F32))
         keep(i, 1, jnp.dot(tok[...], wgu[i, 1], preferred_element_type=F32))
+        chunk(i - n + soon, lambda c, _: act_copy(0, c, 1).start())
         bottom(i)
         return 0
 
@@ -327,32 +374,56 @@
     def b_bottom(m):
         group(m - 2, lambda g, i: chip_sum(1, g, i))
 
+    def hidden_of(m, do):
+        for i in range(2):
+            chunk(soon + 2 * m + i, do)
+
+    def last_hidden(m, do):
+        chunk(soon + 2 * groups + m, do)
+
     def backward(m, cs):
-        top(n + m)
+        @pl.when(m == 0)
+        def _():
+            pair_copy(0, n - 1, 1).start()
+            far_start(0, n - 3, 1)
+
+        @pl.when(m == 1)
+        def _():
+            far_start(0, n - 2, 1)
+            far_start(0, n - 1, 1)
+
         b_top(m)
-        activate(0, m, 1)
+        hidden_of(m, lambda c, _: activate(0, c, 1))
         load_d(m, cs[0], len(cs)).wait()
         for c in cs:
             keep(c, 2, lax.dot_general(cot[...], wd_of(c), NT, preferred_element_type=F32))
-        act_copy(0, m, 1).start()
-        bottom(n + m)
+        hidden_of(m, lambda c, _: act_copy(0, c, 1).start())
+        @pl.when(m == 0)
+        def _():
+            chip_sum(0, n - 2, 1)
+            chip_sum(0, n - 1, 1)
+
         b_bottom(m)
 
-    grouped(two, backward)
+    grouped(backward)
+
+    early = max(0, groups - 2)
 
     def mix(m, cs):
         b_top(groups + m)
-        chunk(groups + m, lambda c, i: activate(0, c, i))
+        last_hidden(m, lambda c, _: activate(0, c, 1))
+        group(m - (groups - early), lambda g, i: activate(1, g, i))
         for c in cs:
             act_wait(0, c, 1)
         acc = 0.0
         for c in cs:
             acc = acc + jnp.dot(lhs(c, 0), wd_of(c), preferred_element_type=F32)
         mixed[...] += acc
-        chunk(groups + m, lambda c, i: act_copy(0, c, i).start())
+        last_hidden(m, lambda c, _: act_copy(0, c, 1).start())
+        group(m - (groups - early), lambda g, i: act_copy(1, g, i).start())
         b_bottom(groups + m)
 
-    grouped(two, mix)
+    grouped(mix)
 
     def add_grad(lo, hi, cs):
         acc = 0.0
@@ -361,55 +432,49 @@
             acc = acc + lax.dot_general(lhs(c, 2), wgu[c, 1, lo:hi, :], NT, preferred_element_type=F32)
         grad[:, lo:hi] += acc
 
-    ahead = 2
-    for g in range(ahead):
-        activate(1, g, two)
     y_stage(0)
-    for g in range(ahead):
-        act_copy(1, g, two).start()
 
     def grad_a(m, cs):
-        at(m, two, 0, lambda: y_copy(0).start())
-        at(m, two, 5, lambda: z_stage(0, 0))
-        at(m, two, 6, lambda: z_start(0, 0))
-        group(m + ahead, lambda g, i: activate(1, g, i))
+        at(m, 0, lambda: y_copy(0).start())
+        at(m, 3, lambda: z_stage(0, 0))
+        group(m + early, lambda g, i: activate(1, g, i))
         act_wait(1, m, len(cs))
         add_grad(0, 2 * pw, cs)
-        group(m + ahead, lambda g, i: act_copy(1, g, i).start())
-
-    grouped(two, grad_a)
+        group(m + early, lambda g, i: act_copy(1, g, i).start())
+
+    grouped(grad_a)
+    z_start(0, 0)
     y_stage(1)
 
     def grad_b(m, cs):
-        at(m, four, 0, lambda: y_copy(1).start())
-        at(m, four, 2, lambda: z_stage(0, 1))
-        at(m, four, 3, lambda: z_start(0, 1))
+        at(m, 0, lambda: y_copy(1).start())
         add_grad(2 * pw, 3 * pw, cs)
 
-    grouped(four, grad_b)
+    grouped(grad_b)
     y_stage(2)
 
     def grad_c(m, cs):
-        at(m, four, 0, lambda: y_copy(2).start())
-        at(m, four, 1, lambda: z_stage(1, 0))
-        at(m, four, 2, lambda: z_start(1, 0))
+        at(m, 0, lambda: y_copy(2).start())
+        at(m, 1, lambda: z_stage(0, 1))
+        at(m, 2, lambda: z_start(0, 1))
+        at(m, 2, lambda: z_stage(1, 0))
+        at(m, 3, lambda: z_start(1, 0))
         add_grad(3 * pw, depth, cs)
 
-    grouped(four, grad_c)
-    y_stage(3)
-    y_copy(3).start()
+    grouped(grad_c)
+    last_stage()
     z_step(2, 0)
+    for e in range(2 * nb - 1, 0, -1):
+        last_copy(e).start()
     z_step(1, 1)
+    z_step(2, 1)
     z_step(0, 2)
-    z_step(2, 1)
-    z_step(3, 0)
     z_step(1, 2)
-    z_step(3, 1)
     z_step(2, 2)
-    z_step(3, 2)
     for s in range(3, steps + 1):
         for o in range(len(outs)):
             z_step(o, s)
+    last_sum()
 
 
     def left(ref, sem):
@@ -425,6 +490,7 @@
     left(ysend, y_send.at[0])
     for s in range(steps):
         left(zsend.at[:, pl.ds(z_base(s), span(s))], z_send.at[s])
+    left(lsend, l_send.at[0])
 
 
 def per_device(ng, nb, nu, tokens, cotangent, gate_weight, up_weight, down_weight):
@@ -442,6 +508,8 @@
     steps = nb.bit_length() - 1
     fold = next((f for f in (1, 2, 4, 8) if rows * f % 8 == 0 and depth % (256 * f) == 0), 1)
     wide = depth // (2 * fold)
+    zfold = next((f for f in (1, 2, 4) if rows * f % 8 == 0 and pw % (128 * f) == 0), 1)
+    zwide = pw // zfold
     dma = pltpu.SemaphoreType.DMA
     vm = pltpu.VMEM
     both = pl.pallas_call(
@@ -456,11 +524,14 @@
             vm((n, 2, 3, half, fc), F32), vm((n, 3, half, fc), F32), vm((n, 3, half, fc), BF),
             vm((chips - 1, n, 3, half, fc), BF), vm((n, 2, half, fc), F32), vm((n, 2, 3, half, fc), BF),
             vm((t, depth), F32), vm((t, depth), F32),
-            vm((2 * PARTS, half, pw), BF), vm((2 * PARTS, half, pw), BF), vm((2 * PARTS, half, pw), F32),
-            vm((2 * PARTS, nb - 1, rows, pw), BF), vm((2 * PARTS, nb - 1, rows, pw), BF),
-            dma((n,)), dma((pl.cdiv(n, 2),)), dma((2,)), dma((2,)), dma((2, 2 * nb, 2)),
+            vm((2 * PARTS - 1, half, pw), BF), vm((2 * PARTS - 1, half, pw), BF), vm((2 * PARTS - 1, half, pw), F32),
+            vm((2 * PARTS - 1, nb // 2, rows * zfold, zwide), F32),
+            vm((2 * PARTS - 1, nb - 1, rows * zfold, zwide), BF), vm((2 * PARTS - 1, nb - 1, rows * zfold, zwide), BF),
+            vm((2 * nb - 1, rows * zfold, zwide), F32), vm((2 * nb - 1, rows * zfold, zwide), BF),
+            vm((2 * nb - 1, rows * zfold, zwide), BF),
+            dma((n,)), dma((pl.cdiv(n, SIZE),)), dma((2,)), dma((2,)), dma((2, 2 * nb, 2)),
             dma((2,)), dma((2, n)), dma((2, chips - 1)), dma((2, n, chips - 1)), dma((2,)), dma((2, n)),
-            dma((1,)), dma((PARTS,)), dma((steps,)), dma((PARTS, steps)),
+            dma((1,)), dma((3,)), dma((steps,)), dma((3, steps)), dma((1,)), dma((2 * nb - 1,)),
         ],
         compiler_params=pltpu.CompilerParams(
             collective_id=0, has_side_effects=True, vmem_limit_bytes=67043328 - 4 * depth * pl.cdiv(rows, 16) * 16),

time: 61.1 us -> 56.2 us (0.920)
  Pallas kernels: 59.6 us -> 54.7 us
    pallas_call x1, Pallas kernels: 59.6 us -> 54.7 us  [per_device(): pl.pallas_call(functools.partial(kernel, nb, nu, n, total, fc), out_shape...]
where the time goes in v4:
time: 56.2 us; the launch traced here: 56 us
  Pallas kernels  54.7 us (97%)
  local copies, waits for them, and re-layouts  0.66 us (1%)
  between operations  0.64 us (1%)
    pallas_call x1, Pallas kernels, per_device(): pl.pallas_call(functools.partial(kernel, nb, nu, n, total, fc), out_shape...  54.7 us

profile of v4, /device:TPU:0, one launch (start us, length us, event | category | flops | bytes accessed | tf_op | source)
XLA Modules:
  0.0 56.0 jit_solution(17319718190609668173)
XLA Ops:
  0.6 54.7 %shard_map.68 = bf16[2,10,2048]{2,1,0:T(8,128)(2,1)S(1)} custom-call(bf16[10,2048]{1,0:T(8,128)(2,1)} %tok_in.1, bf16[10,2048]{1,0:T(8,128)(2,1)} %cot_in.1, bf16[2048,6656]{1,0:T(8,128)(2,1)} %wg_hbm.1, bf16[2048,6656]{1,0:T(8,128)(2,1)} %wu_hbm.1, bf16[6656,2048]{1,0:T(8,128)(2,1)} %wd_hbm.1), custom_call_target="tpu_custom_call" | custom-call | tf_op jit(solution)/shard_map/pallas_call | solution.py:515
  55.4 0.7 %slice_bitcast_fusion = (bf16[10,2048]{1,0:T(8,128)(2,1)}, bf16[10,2048]{1,0:T(8,128)(2,1)}) fusion(bf16[2,10,2048]{2,1,0:T(8,128)(2,1)S(1)} %shard_map.68), kind=kLoop, calls=%fused_computation | loop fusion | bytes 163840 | tf_op jit(solution)/shard_map/squeeze | solution.py:539

commit v5 on v4

--- a/solution.py
+++ b/solution.py
@@ -12,7 +12,12 @@
 F32 = jnp.float32
 NT = (((1,), (1,)), ((), ()))
 PARTS = 4
-SIZE = 4
+LEAD = 5
+SOON = 4
+
+
+def chunks_at_once(n):
+    return next(s for s in (4, 2) if n // s >= 3)
 
 
 def flip(i, m):
@@ -27,7 +32,7 @@
 
 
 def kernel(nb, nu, n, total, fc, tok_in, cot_in, wg_hbm, wu_hbm, wd_hbm, out,
-           wgu, wd, own, folded, got, tok, cot, part, pair, chip, far, coef, act,
+           wgu, wd, own, folded, got, tokh, tok, cot, part, pair, chip, far, coef, act,
            mixed, grad, ysend, yrecv, ysum, zflat, zsend, zrecv, lflat, lsend, lrecv,
            gu_sem, d_sem, own_sem, tk_send, tk_recv, p_send, p_recv,
            f_send, f_recv, a_send, a_recv, y_send, y_recv, z_send, z_recv, l_send, l_recv):
@@ -39,8 +44,11 @@
     rows, depth = tok_in.shape
     half = nb * rows
     pw = depth // PARTS
-    size = SIZE
-    groups = pl.cdiv(n, size)
+    size = chunks_at_once(n)
+    groups = n // size
+    rest = size + n % size
+    lead = min(LEAD, n - 3)
+    soon = min(SOON, lead)
     steps = nb.bit_length() - 1
     bits = [1 << s for s in range(steps)]
     first_chunk = jnp.minimum(g_me * n, total - n)
@@ -120,15 +128,14 @@
                 folded[w, h, j * rows:(j + 1) * rows, :] = own[w, :, place(h, j)].astype(F32)
         got[w, 0] = folded[w].astype(BF)
 
-    def pack(w, scratch, dst):
-        for e in range(2 * nb):
+    def pack(w, other, scratch):
+        for e in range(other * nb, (other + 1) * nb):
             for h in range(2):
-                if e >= nb:
+                if other:
                     tok_wait(w, e, h)
                 for j in range(fold):
                     scratch[e * rows:(e + 1) * rows, place(h, j)] = (
                         got[w, e, h, j * rows:(j + 1) * rows, :].astype(F32))
-        dst[...] = scratch[...].astype(BF)
 
 
     def js(t):
@@ -296,14 +303,15 @@
         pl.when(valid(c))(lambda: f(c, 1))
 
     def group(m, f):
-        pl.when(jnp.logical_and(m >= 0, m < n // size))(lambda: f(m, size))
-        if n % size:
-            pl.when(m == n // size)(lambda: f(n // size, n % size))
+        pl.when(jnp.logical_and(m >= 0, m < groups - 1))(lambda: f(m, size))
+        pl.when(m == groups - 1)(lambda: f(groups - 1, rest))
+
+    def small_then_last(m, f):
+        group(jnp.where(m < groups - 1, m, jnp.where(m == groups - 1, -1, m - 1)), f)
 
     def grouped(f):
-        lax.fori_loop(0, n // size, lambda m, _: f(m, [m * size + i for i in range(size)]) or 0, 0)
-        if n % size:
-            f(jnp.int32(n // size), list(range(n - n % size, n)))
+        lax.fori_loop(0, groups - 1, lambda m, _: f(m, [m * size + i for i in range(size)]) or 0, 0)
+        f(jnp.int32(groups - 1), list(range(n - rest, n)))
 
     def at(m, k, f):
         pl.when(m == min(k, groups - 1))(f)
@@ -317,11 +325,11 @@
         own_copy(w).start()
     for w in range(2):
         fold_own(w)
-    for c in range(n):
+    for c in (*range(n - lead, n), *range(n - lead)):
         for cp in load_gu(c):
             cp.start()
     for m in range(groups):
-        load_d(m, m * size, min(size, n - m * size)).start()
+        load_d(m, m * size, size if m < groups - 1 else rest).start()
     pl.semaphore_wait(barrier, len(peers))
 
     for w in range(2):
@@ -330,67 +338,94 @@
         tok_forward(0, e)
     for e in range(1, nb - 1):
         tok_forward(1, e)
-    pack(0, mixed, tok)
+
+
+    def done(t, h):
+        whole = t - lead
+        return jnp.where(h == 0, jnp.where(t < 0, -1, jnp.where(t < lead, n - lead + t, jnp.where(t < n, whole, -1))),
+                         whole)
 
     def top(t):
-        chunk(t - 1, lambda c, i: pair_copy(0, c, i).start())
-        chunk(t - 3, lambda c, i: far_start(0, c, i))
+        chunk(done(t - 1, 1 - k_me), lambda c, i: pair_copy(0, c, i).start())
+        chunk(done(t - 3, k_me), lambda c, i: far_start(0, c, i))
 
     def bottom(t):
-        chunk(t - 2, lambda c, i: chip_sum(0, c, i))
+        chunk(done(t - 2, k_me), lambda c, i: chip_sum(0, c, i))
 
     def keep(c, j, v):
         part[c, 0, j] = v[:half]
         part[c, 1, j] = v[half:]
 
-
-    soon = max(0, n - 10)
-
-    def forward(i, _):
-        top(i)
-        chunk(i - n + soon, lambda c, _: activate(0, c, 1))
-
-        @pl.when(i == min(7, n - 1))
+    def rows_first(other, t, _):
+        top(t)
+        ready = t - n - lead + soon
+        if other:
+            chunk(ready, lambda c, _: activate(0, c, 1))
+        c = t - lead if other else t + n - lead
+        if not other:
+            wait_gu(c)
+        for j in range(2):
+            part[c, other, j] = jnp.dot(tokh[other], wgu[c, j], preferred_element_type=F32)
+        if other:
+            chunk(ready, lambda c, _: act_copy(0, c, 1).start())
+        bottom(t)
+        return 0
+
+    def forward(t, _):
+        top(t)
+        @pl.when(t == lead + 3)
         def _():
             tok_forward(1, nb - 1)
 
+        i = t - lead
         wait_gu(i)
         keep(i, 0, jnp.dot(tok[...], wgu[i, 0], preferred_element_type=F32))
         keep(i, 1, jnp.dot(tok[...], wgu[i, 1], preferred_element_type=F32))
-        chunk(i - n + soon, lambda c, _: act_copy(0, c, 1).start())
-        bottom(i)
+        bottom(t)
         return 0
 
-    lax.fori_loop(0, n, forward, 0)
-    pack(1, grad, cot)
+    pack(0, 0, mixed)
+    tokh[0] = mixed[:half].astype(BF)
+    lax.fori_loop(0, lead, functools.partial(rows_first, 0), 0)
+    pack(0, 1, mixed)
+    tokh[1] = mixed[half:].astype(BF)
+    tok[...] = mixed[...].astype(BF)
+    lax.fori_loop(lead, n, forward, 0)
+    lax.fori_loop(n, n + lead, functools.partial(rows_first, 1), 0)
+    for other in range(2):
+        pack(1, other, grad)
+    cot[...] = grad[...].astype(BF)
     mixed[...] = jnp.zeros_like(mixed)
     grad[...] = jnp.zeros_like(grad)
 
 
     def b_top(m):
         group(m - 1, lambda g, i: pair_copy(1, g, i).start())
-        group(m - 3, lambda g, i: far_start(1, g, i))
+        small_then_last(m - 2, lambda g, i: far_start(1, g, i))
 
     def b_bottom(m):
-        group(m - 2, lambda g, i: chip_sum(1, g, i))
+        small_then_last(m - 1, lambda g, i: chip_sum(1, g, i))
 
     def hidden_of(m, do):
-        for i in range(2):
-            chunk(soon + 2 * m + i, do)
+        chunk(soon + m, do)
+        if soon + groups < n:
+            pl.when(m == groups - 1)(lambda: do(soon + groups, 1))
 
     def last_hidden(m, do):
-        chunk(soon + 2 * groups + m, do)
+        @pl.when(m == 0)
+        def _():
+            for c in range(soon + groups + 1, n):
+                do(c, 1)
 
     def backward(m, cs):
         @pl.when(m == 0)
         def _():
-            pair_copy(0, n - 1, 1).start()
-            far_start(0, n - 3, 1)
+            top(n + lead)
 
         @pl.when(m == 1)
         def _():
-            far_start(0, n - 2, 1)
-            far_start(0, n - 1, 1)
+            for t in (n + lead + 1, n + lead + 2):
+                chunk(done(t - 3, k_me), lambda c, i: far_start(0, c, i))
 
         b_top(m)
         hidden_of(m, lambda c, _: activate(0, c, 1))
@@ -400,14 +435,14 @@
         hidden_of(m, lambda c, _: act_copy(0, c, 1).start())
         @pl.when(m == 0)
         def _():
-            chip_sum(0, n - 2, 1)
-            chip_sum(0, n - 1, 1)
+            bottom(n + lead)
+            bottom(n + lead + 1)
 
         b_bottom(m)
 
     grouped(backward)
 
-    early = max(0, groups - 2)
+    early = 1
 
     def mix(m, cs):
         b_top(groups + m)
@@ -415,12 +450,17 @@
         group(m - (groups - early), lambda g, i: activate(1, g, i))
         for c in cs:
             act_wait(0, c, 1)
-        acc = 0.0
-        for c in cs:
-            acc = acc + jnp.dot(lhs(c, 0), wd_of(c), preferred_element_type=F32)
-        mixed[...] += acc
+        def add(cs):
+            acc = 0.0
+            for c in cs:
+                acc = acc + jnp.dot(lhs(c, 0), wd_of(c), preferred_element_type=F32)
+            mixed[...] += acc
+
+        add(cs[:2])
         last_hidden(m, lambda c, _: act_copy(0, c, 1).start())
         group(m - (groups - early), lambda g, i: act_copy(1, g, i).start())
+        if cs[2:]:
+            add(cs[2:])
         b_bottom(groups + m)
 
     grouped(mix)
@@ -436,11 +476,12 @@
 
     def grad_a(m, cs):
         at(m, 0, lambda: y_copy(0).start())
-        at(m, 3, lambda: z_stage(0, 0))
+        at(m, 2, lambda: z_stage(0, 0))
         group(m + early, lambda g, i: activate(1, g, i))
         act_wait(1, m, len(cs))
-        add_grad(0, 2 * pw, cs)
+        add_grad(0, 2 * pw, cs[:1])
         group(m + early, lambda g, i: act_copy(1, g, i).start())
+        add_grad(0, 2 * pw, cs[1:])
 
     grouped(grad_a)
     z_start(0, 0)
@@ -455,10 +496,10 @@
 
     def grad_c(m, cs):
         at(m, 0, lambda: y_copy(2).start())
-        at(m, 1, lambda: z_stage(0, 1))
+        at(m, 2, lambda: z_stage(1, 0))
+        at(m, 2, lambda: z_stage(0, 1))
+        at(m, 2, lambda: z_start(1, 0))
         at(m, 2, lambda: z_start(0, 1))
-        at(m, 2, lambda: z_stage(1, 0))
-        at(m, 3, lambda: z_start(1, 0))
         add_grad(3 * pw, depth, cs)
 
     grouped(grad_c)
@@ -520,7 +561,8 @@
         scratch_shapes=[
             vm((n, 2, depth, fc), BF), vm((n * fc, depth), BF),
             vm((2, rows, depth), BF), vm((2, 2, rows * fold, wide), F32),
-            vm((2, 2 * nb, 2, rows * fold, wide), BF), vm((t, depth), BF), vm((t, depth), BF),
+            vm((2, 2 * nb, 2, rows * fold, wide), BF),
+            vm((2, half, depth), BF), vm((t, depth), BF), vm((t, depth), BF),
             vm((n, 2, 3, half, fc), F32), vm((n, 3, half, fc), F32), vm((n, 3, half, fc), BF),
             vm((chips - 1, n, 3, half, fc), BF), vm((n, 2, half, fc), F32), vm((n, 2, 3, half, fc), BF),
             vm((t, depth), F32), vm((t, depth), F32),
@@ -529,7 +571,7 @@
             vm((2 * PARTS - 1, nb - 1, rows * zfold, zwide), BF), vm((2 * PARTS - 1, nb - 1, rows * zfold, zwide), BF),
             vm((2 * nb - 1, rows * zfold, zwide), F32), vm((2 * nb - 1, rows * zfold, zwide), BF),
             vm((2 * nb - 1, rows * zfold, zwide), BF),
-            dma((n,)), dma((pl.cdiv(n, SIZE),)), dma((2,)), dma((2,)), dma((2, 2 * nb, 2)),
+            dma((n,)), dma((n // chunks_at_once(n),)), dma((2,)), dma((2,)), dma((2, 2 * nb, 2)),
             dma((2,)), dma((2, n)), dma((2, chips - 1)), dma((2, n, chips - 1)), dma((2,)), dma((2, n)),
             dma((1,)), dma((3,)), dma((steps,)), dma((3, steps)), dma((1,)), dma((2 * nb - 1,)),
         ],

time: 56.2 us -> 53.6 us (0.954)
  Pallas kernels: 54.7 us -> 52.1 us
    pallas_call x1, Pallas kernels: 54.7 us -> 52.1 us  [per_device(): pl.pallas_call(functools.partial(kernel, nb, nu, n, total, fc), out_shape...]
where the time goes in v5:
time: 53.6 us; the launch traced here: 53.4 us
  Pallas kernels  52.1 us (97%)
  local copies, waits for them, and re-layouts  0.66 us (1%)
  between operations  0.64 us (1%)
    pallas_call x1, Pallas kernels, per_device(): pl.pallas_call(functools.partial(kernel, nb, nu, n, total, fc), out_shape...  52.1 us

profile of v5, /device:TPU:0, one launch (start us, length us, event | category | flops | bytes accessed | tf_op | source)
XLA Modules:
  0.0 53.4 jit_solution(9095563240717578524)
XLA Ops:
  0.6 52.1 %shard_map.68 = bf16[2,10,2048]{2,1,0:T(8,128)(2,1)S(1)} custom-call(bf16[10,2048]{1,0:T(8,128)(2,1)} %tok_in.1, bf16[10,2048]{1,0:T(8,128)(2,1)} %cot_in.1, bf16[2048,6656]{1,0:T(8,128)(2,1)} %wg_hbm.1, bf16[2048,6656]{1,0:T(8,128)(2,1)} %wu_hbm.1, bf16[6656,2048]{1,0:T(8,128)(2,1)} %wd_hbm.1), custom_call_target="tpu_custom_call" | custom-call | tf_op jit(solution)/shard_map/pallas_call | solution.py:556
  52.7 0.7 %slice_bitcast_fusion = (bf16[10,2048]{1,0:T(8,128)(2,1)}, bf16[10,2048]{1,0:T(8,128)(2,1)}) fusion(bf16[2,10,2048]{2,1,0:T(8,128)(2,1)S(1)} %shard_map.68), kind=kLoop, calls=%fused_computation | loop fusion | bytes 163840 | tf_op jit(solution)/shard_map/squeeze | solution.py:581

commit v6 on v5

--- a/solution.py
+++ b/solution.py
@@ -13,7 +13,6 @@
 NT = (((1,), (1,)), ((), ()))
 PARTS = 4
 LEAD = 5
-SOON = 4
 
 
 def chunks_at_once(n):
@@ -47,8 +46,8 @@
     size = chunks_at_once(n)
     groups = n // size
     rest = size + n % size
-    lead = min(LEAD, n - 3)
-    soon = min(SOON, lead)
+    lead = min(LEAD, n - 4)
+    pre = 0
     steps = nb.bit_length() - 1
     bits = [1 << s for s in range(steps)]
     first_chunk = jnp.minimum(g_me * n, total - n)
@@ -141,8 +140,11 @@
     def js(t):
         return pl.ds(0, 2) if t == 0 else pl.ds(2, 1)
 
+    def start_of(m):
+        return 0 if isinstance(m, int) and m == 0 else m * size + n % size
+
     def rows_of(t, m, cnt):
-        return pl.ds(m if t == 0 else m * size, cnt)
+        return pl.ds(m if t == 0 else start_of(m), cnt)
 
     def pair_copy(t, m, cnt):
         r = rows_of(t, m, cnt)
@@ -151,7 +153,7 @@
     def chip_sum(t, m, cnt):
         pair_copy(t, m, cnt).wait_recv()
         for i in range(cnt):
-            c = m if t == 0 else m * size + i
+            c = m if t == 0 else start_of(m) + i
             for j in ((0, 1), (2,))[t]:
                 chip[c, j] = (part[c, k_me, j] + pair[c, j]).astype(BF)
 
@@ -168,7 +170,7 @@
         for d in range(1, chips):
             far_copy(t, m, cnt, d).wait_recv()
         for i in range(cnt):
-            values(t, m if t == 0 else m * size + i)
+            values(t, m if t == 0 else start_of(m) + i)
 
     def values(t, c):
         def total_of(j):
@@ -210,7 +212,7 @@
         return jnp.concatenate([act[c, 0, j].astype(F32), act[c, 1, j].astype(F32)], axis=0).astype(BF)
 
 
-    outs = [(0, PARTS), (PARTS, 2), (PARTS + 2, 1)]
+    outs = [(0, PARTS // 2), (PARTS // 2, PARTS // 2), (PARTS, 2)]
 
     def acc_of(q):
         acc = mixed if q < PARTS else grad
@@ -275,25 +277,31 @@
     def last_peer(e):
         return {"grp": flip(g_me, 1) if e >= nb else g_me, "blk": flips(b_me, e % nb)}
 
-    def last_stage():
+    def last_cols(d, j):
+        lo = depth - (2 - d) * pw + j * zwide
+        return slice(lo, lo + zwide)
+
+    def last_stage(d):
         for e in range(1, 2 * nb):
             for j in range(zfold):
-                lflat[e - 1, j * rows:(j + 1) * rows, :] = (
-                    grad[e * rows:(e + 1) * rows, depth - pw + j * zwide:depth - pw + (j + 1) * zwide])
-        lsend[...] = lflat[...].astype(BF)
-
-    def last_copy(e):
-        return rcopy(lsend.at[e - 1], lrecv.at[e - 1], l_send.at[0], l_recv.at[e - 1], last_peer(e))
-
-    def last_sum():
+                lflat[d, e - 1, j * rows:(j + 1) * rows, :] = grad[e * rows:(e + 1) * rows, last_cols(d, j)]
+        lsend[d] = lflat[d].astype(BF)
+
+    def last_copy(d, e):
+        return rcopy(lsend.at[d, e - 1], lrecv.at[d, e - 1], l_send.at[0], l_recv.at[d, e - 1], last_peer(e))
+
+    def last_start(d):
+        for e in range(2 * nb - 1, 0, -1):
+            last_copy(d, e).start()
+
+    def last_sum(d):
         for e in range(1, 2 * nb):
-            last_copy(e).wait_recv()
+            last_copy(d, e).wait_recv()
         for j in range(zfold):
-            lo = depth - pw + j * zwide
-            v = grad[:rows, lo:lo + zwide]
+            v = grad[:rows, last_cols(d, j)]
             for e in range(1, 2 * nb):
-                v = v + lrecv[e - 1, j * rows:(j + 1) * rows, :].astype(F32)
-            out[1, :, lo:lo + zwide] = v.astype(BF)
+                v = v + lrecv[d, e - 1, j * rows:(j + 1) * rows, :].astype(F32)
+            out[1, :, last_cols(d, j)] = v.astype(BF)
 
 
     def valid(c):
@@ -302,16 +310,13 @@
     def chunk(c, f):
         pl.when(valid(c))(lambda: f(c, 1))
 
-    def group(m, f):
-        pl.when(jnp.logical_and(m >= 0, m < groups - 1))(lambda: f(m, size))
-        pl.when(m == groups - 1)(lambda: f(groups - 1, rest))
-
-    def small_then_last(m, f):
-        group(jnp.where(m < groups - 1, m, jnp.where(m == groups - 1, -1, m - 1)), f)
-
-    def grouped(f):
-        lax.fori_loop(0, groups - 1, lambda m, _: f(m, [m * size + i for i in range(size)]) or 0, 0)
-        f(jnp.int32(groups - 1), list(range(n - rest, n)))
+    def later_group(m, f):
+        pl.when(jnp.logical_and(m >= 1, m < groups))(lambda: f(m, size))
+
+    def grouped(f, start=0):
+        if start == 0:
+            f(0, list(range(rest)))
+        lax.fori_loop(1, groups, lambda m, _: f(m, [start_of(m) + i for i in range(size)]) or 0, 0)
 
     def at(m, k, f):
         pl.when(m == min(k, groups - 1))(f)
@@ -329,7 +334,7 @@
         for cp in load_gu(c):
             cp.start()
     for m in range(groups):
-        load_d(m, m * size, size if m < groups - 1 else rest).start()
+        load_d(m, start_of(m), size if m else rest).start()
     pl.semaphore_wait(barrier, len(peers))
 
     for w in range(2):
@@ -358,8 +363,10 @@
 
     def rows_first(other, t, _):
         top(t)
-        ready = t - n - lead + soon
+        ready = jnp.where(t < n + pre, t - n, jnp.where(t < n + lead - 1, t - n + 1, -1))
         if other:
+            pl.when(t == n + pre)(lambda: pair_copy(1, 0, rest).start())
+            pl.when(t == n + lead - 1)(lambda: far_start(1, 0, rest))
             chunk(ready, lambda c, _: activate(0, c, 1))
         c = t - lead if other else t + n - lead
         if not other:
@@ -368,12 +375,13 @@
             part[c, other, j] = jnp.dot(tokh[other], wgu[c, j], preferred_element_type=F32)
         if other:
             chunk(ready, lambda c, _: act_copy(0, c, 1).start())
+            pl.when(t == n + lead - 2)(lambda: chip_sum(1, 0, rest))
         bottom(t)
         return 0
 
     def forward(t, _):
         top(t)
-        @pl.when(t == lead + 3)
+        @pl.when(t == lead)
         def _():
             tok_forward(1, nb - 1)
 
@@ -391,7 +399,7 @@
     tokh[1] = mixed[half:].astype(BF)
     tok[...] = mixed[...].astype(BF)
     lax.fori_loop(lead, n, forward, 0)
-    lax.fori_loop(n, n + lead, functools.partial(rows_first, 1), 0)
+    lax.fori_loop(n, n + pre, functools.partial(rows_first, 1), 0)
     for other in range(2):
         pack(1, other, grad)
     cot[...] = grad[...].astype(BF)
@@ -400,67 +408,71 @@
 
 
     def b_top(m):
-        group(m - 1, lambda g, i: pair_copy(1, g, i).start())
-        small_then_last(m - 2, lambda g, i: far_start(1, g, i))
+        later_group(m - 1, lambda g, i: pair_copy(1, g, i).start())
+        later_group(m - 2, lambda g, i: far_start(1, g, i))
 
     def b_bottom(m):
-        small_then_last(m - 1, lambda g, i: chip_sum(1, g, i))
+        later_group(m - 1, lambda g, i: chip_sum(1, g, i))
+
+    base = lead + 1 + 2 * (groups - 2)
 
     def hidden_of(m, do):
-        chunk(soon + m, do)
-        if soon + groups < n:
-            pl.when(m == groups - 1)(lambda: do(soon + groups, 1))
+        pl.when(m == 1)(lambda: do(lead, 1))
+        for i in range(2):
+            pl.when(m > 1)(lambda i=i: do(lead + 1 + 2 * (m - 2) + i, 1))
 
     def last_hidden(m, do):
-        @pl.when(m == 0)
-        def _():
-            for c in range(soon + groups + 1, n):
-                do(c, 1)
+        for k, cs in enumerate((range(base, min(base + 3, n)), range(base + 3, n))):
+            @pl.when(m == k)
+            def _():
+                for c in cs:
+                    do(c, 1)
+
+    def back_dots(m, cs):
+        load_d(m, cs[0], len(cs)).wait()
+        for c in cs:
+            keep(c, 2, lax.dot_general(cot[...], wd_of(c), NT, preferred_element_type=F32))
 
     def backward(m, cs):
-        @pl.when(m == 0)
+        @pl.when(m == 1)
         def _():
             top(n + lead)
 
-        @pl.when(m == 1)
+        @pl.when(m == 2)
         def _():
             for t in (n + lead + 1, n + lead + 2):
                 chunk(done(t - 3, k_me), lambda c, i: far_start(0, c, i))
 
         b_top(m)
         hidden_of(m, lambda c, _: activate(0, c, 1))
-        load_d(m, cs[0], len(cs)).wait()
-        for c in cs:
-            keep(c, 2, lax.dot_general(cot[...], wd_of(c), NT, preferred_element_type=F32))
+        back_dots(m, cs)
         hidden_of(m, lambda c, _: act_copy(0, c, 1).start())
-        @pl.when(m == 0)
+
+        @pl.when(m == 1)
         def _():
             bottom(n + lead)
             bottom(n + lead + 1)
 
         b_bottom(m)
 
-    grouped(backward)
-
-    early = 1
+    activate(0, pre, 1)
+    back_dots(0, list(range(rest)))
+    act_copy(0, pre, 1).start()
+    lax.fori_loop(n + pre, n + lead, functools.partial(rows_first, 1), 0)
+    grouped(backward, 1)
 
     def mix(m, cs):
         b_top(groups + m)
         last_hidden(m, lambda c, _: activate(0, c, 1))
-        group(m - (groups - early), lambda g, i: activate(1, g, i))
+        pl.when(m == groups - 1)(lambda: activate(1, 0, rest))
         for c in cs:
             act_wait(0, c, 1)
-        def add(cs):
-            acc = 0.0
-            for c in cs:
-                acc = acc + jnp.dot(lhs(c, 0), wd_of(c), preferred_element_type=F32)
-            mixed[...] += acc
-
-        add(cs[:2])
         last_hidden(m, lambda c, _: act_copy(0, c, 1).start())
-        group(m - (groups - early), lambda g, i: act_copy(1, g, i).start())
-        if cs[2:]:
-            add(cs[2:])
+        pl.when(m == groups - 1)(lambda: act_copy(1, 0, rest).start())
+        acc = 0.0
+        for c in cs:
+            acc = acc + jnp.dot(lhs(c, 0), wd_of(c), preferred_element_type=F32)
+        mixed[...] += acc
         b_bottom(groups + m)
 
     grouped(mix)
@@ -473,49 +485,47 @@
         grad[:, lo:hi] += acc
 
     y_stage(0)
+    y_stage(1)
 
     def grad_a(m, cs):
         at(m, 0, lambda: y_copy(0).start())
-        at(m, 2, lambda: z_stage(0, 0))
-        group(m + early, lambda g, i: activate(1, g, i))
+        at(m, 1, lambda: y_copy(1).start())
+        at(m, 2, lambda: z_step(0, 0))
+        later_group(m + 1, lambda g, i: activate(1, g, i))
         act_wait(1, m, len(cs))
-        add_grad(0, 2 * pw, cs[:1])
-        group(m + early, lambda g, i: act_copy(1, g, i).start())
-        add_grad(0, 2 * pw, cs[1:])
+        later_group(m + 1, lambda g, i: act_copy(1, g, i).start())
+        add_grad(0, 2 * pw, cs)
 
     grouped(grad_a)
-    z_start(0, 0)
-    y_stage(1)
+    y_stage(2)
 
     def grad_b(m, cs):
-        at(m, 0, lambda: y_copy(1).start())
+        at(m, 0, lambda: y_copy(2).start())
+        at(m, 0, lambda: z_step(1, 0))
+        at(m, 2, lambda: z_step(0, 1))
         add_grad(2 * pw, 3 * pw, cs)
 
     grouped(grad_b)
-    y_stage(2)
+    last_stage(0)
 
     def grad_c(m, cs):
-        at(m, 0, lambda: y_copy(2).start())
-        at(m, 2, lambda: z_stage(1, 0))
-        at(m, 2, lambda: z_stage(0, 1))
-        at(m, 2, lambda: z_start(1, 0))
-        at(m, 2, lambda: z_start(0, 1))
+        at(m, 0, lambda: last_start(0))
+        at(m, 1, lambda: z_step(1, 1))
+        at(m, 1, lambda: z_step(2, 0))
         add_grad(3 * pw, depth, cs)
 
     grouped(grad_c)
-    last_stage()
-    z_step(2, 0)
-    for e in range(2 * nb - 1, 0, -1):
-        last_copy(e).start()
-    z_step(1, 1)
+    last_stage(1)
+    z_stage(0, 2)
+    last_start(1)
     z_step(2, 1)
-    z_step(0, 2)
     z_step(1, 2)
+    last_sum(0)
     z_step(2, 2)
     for s in range(3, steps + 1):
         for o in range(len(outs)):
             z_step(o, s)
-    last_sum()
+    last_sum(1)
 
 
     def left(ref, sem):
@@ -566,14 +576,14 @@
             vm((n, 2, 3, half, fc), F32), vm((n, 3, half, fc), F32), vm((n, 3, half, fc), BF),
             vm((chips - 1, n, 3, half, fc), BF), vm((n, 2, half, fc), F32), vm((n, 2, 3, half, fc), BF),
             vm((t, depth), F32), vm((t, depth), F32),
-            vm((2 * PARTS - 1, half, pw), BF), vm((2 * PARTS - 1, half, pw), BF), vm((2 * PARTS - 1, half, pw), F32),
-            vm((2 * PARTS - 1, nb // 2, rows * zfold, zwide), F32),
-            vm((2 * PARTS - 1, nb - 1, rows * zfold, zwide), BF), vm((2 * PARTS - 1, nb - 1, rows * zfold, zwide), BF),
-            vm((2 * nb - 1, rows * zfold, zwide), F32), vm((2 * nb - 1, rows * zfold, zwide), BF),
-            vm((2 * nb - 1, rows * zfold, zwide), BF),
+            vm((PARTS + 2, half, pw), BF), vm((PARTS + 2, half, pw), BF), vm((PARTS + 2, half, pw), F32),
+            vm((PARTS + 2, nb // 2, rows * zfold, zwide), F32),
+            vm((PARTS + 2, nb - 1, rows * zfold, zwide), BF), vm((PARTS + 2, nb - 1, rows * zfold, zwide), BF),
+            vm((2, 2 * nb - 1, rows * zfold, zwide), F32), vm((2, 2 * nb - 1, rows * zfold, zwide), BF),
+            vm((2, 2 * nb - 1, rows * zfold, zwide), BF),
             dma((n,)), dma((n // chunks_at_once(n),)), dma((2,)), dma((2,)), dma((2, 2 * nb, 2)),
             dma((2,)), dma((2, n)), dma((2, chips - 1)), dma((2, n, chips - 1)), dma((2,)), dma((2, n)),
-            dma((1,)), dma((3,)), dma((steps,)), dma((3, steps)), dma((1,)), dma((2 * nb - 1,)),
+            dma((1,)), dma((3,)), dma((steps,)), dma((3, steps)), dma((1,)), dma((2, 2 * nb - 1)),
         ],
         compiler_params=pltpu.CompilerParams(
             collective_id=0, has_side_effects=True, vmem_limit_bytes=67043328 - 4 * depth * pl.cdiv(rows, 16) * 16),

time: 53.6 us -> 52.9 us (0.987)
  Pallas kernels: 52.1 us -> 51.5 us
    pallas_call x1, Pallas kernels: 52.1 us -> 51.5 us  [per_device(): pl.pallas_call(functools.partial(kernel, nb, nu, n, total, fc), out_shape...]
where the time goes in v6:
time: 52.9 us; the launch traced here: 52.8 us
  Pallas kernels  51.5 us (97%)
  local copies, waits for them, and re-layouts  0.66 us (1%)
  between operations  0.64 us (1%)
    pallas_call x1, Pallas kernels, per_device(): pl.pallas_call(functools.partial(kernel, nb, nu, n, total, fc), out_shape...  51.5 us

profile of v6, /device:TPU:0, one launch (start us, length us, event | category | flops | bytes accessed | tf_op | source)
XLA Modules:
  0.0 52.8 jit_solution(13520959298298954038)
XLA Ops:
  0.6 51.5 %shard_map.68 = bf16[2,10,2048]{2,1,0:T(8,128)(2,1)S(1)} custom-call(bf16[10,2048]{1,0:T(8,128)(2,1)} %tok_in.1, bf16[10,2048]{1,0:T(8,128)(2,1)} %cot_in.1, bf16[2048,6656]{1,0:T(8,128)(2,1)} %wg_hbm.1, bf16[2048,6656]{1,0:T(8,128)(2,1)} %wu_hbm.1, bf16[6656,2048]{1,0:T(8,128)(2,1)} %wd_hbm.1), custom_call_target="tpu_custom_call" | custom-call | tf_op jit(solution)/shard_map/pallas_call | solution.py:566
  52.1 0.7 %slice_bitcast_fusion = (bf16[10,2048]{1,0:T(8,128)(2,1)}, bf16[10,2048]{1,0:T(8,128)(2,1)}) fusion(bf16[2,10,2048]{2,1,0:T(8,128)(2,1)S(1)} %shard_map.68), kind=kLoop, calls=%fused_computation | loop fusion | bytes 163840 | tf_op jit(solution)/shard_map/squeeze | solution.py:591

commit v7 on v6

--- a/solution.py
+++ b/solution.py
@@ -381,7 +381,7 @@
 
     def forward(t, _):
         top(t)
-        @pl.when(t == lead)
+        @pl.when(t == lead + 1)
         def _():
             tok_forward(1, nb - 1)
 
@@ -422,7 +422,7 @@
             pl.when(m > 1)(lambda i=i: do(lead + 1 + 2 * (m - 2) + i, 1))
 
     def last_hidden(m, do):
-        for k, cs in enumerate((range(base, min(base + 3, n)), range(base + 3, n))):
+        for k, cs in enumerate((range(base + 1, min(base + 4, n)), range(base + 4, n))):
             @pl.when(m == k)
             def _():
                 for c in cs:
@@ -454,6 +454,8 @@
             bottom(n + lead + 1)
 
         b_bottom(m)
+        if base < n:
+            pl.when(m == groups - 1)(lambda: activate(0, base, 1))
 
     activate(0, pre, 1)
     back_dots(0, list(range(rest)))
@@ -463,6 +465,8 @@
 
     def mix(m, cs):
         b_top(groups + m)
+        if base < n:
+            at(m, 0, lambda: act_copy(0, base, 1).start())
         last_hidden(m, lambda c, _: activate(0, c, 1))
         pl.when(m == groups - 1)(lambda: activate(1, 0, rest))
         for c in cs:
@@ -490,7 +494,6 @@
     def grad_a(m, cs):
         at(m, 0, lambda: y_copy(0).start())
         at(m, 1, lambda: y_copy(1).start())
-        at(m, 2, lambda: z_step(0, 0))
         later_group(m + 1, lambda g, i: activate(1, g, i))
         act_wait(1, m, len(cs))
         later_group(m + 1, lambda g, i: act_copy(1, g, i).start())
@@ -501,8 +504,8 @@
 
     def grad_b(m, cs):
         at(m, 0, lambda: y_copy(2).start())
-        at(m, 0, lambda: z_step(1, 0))
-        at(m, 2, lambda: z_step(0, 1))
+        at(m, 0, lambda: z_step(0, 0))
+        at(m, 1, lambda: z_step(1, 0))
         add_grad(2 * pw, 3 * pw, cs)
 
     grouped(grad_b)
@@ -510,15 +513,16 @@
 
     def grad_c(m, cs):
         at(m, 0, lambda: last_start(0))
-        at(m, 1, lambda: z_step(1, 1))
+        at(m, 1, lambda: z_step(0, 1))
         at(m, 1, lambda: z_step(2, 0))
+        at(m, 2, lambda: z_step(1, 1))
         add_grad(3 * pw, depth, cs)
 
     grouped(grad_c)
     last_stage(1)
-    z_stage(0, 2)
     last_start(1)
     z_step(2, 1)
+    z_step(0, 2)
     z_step(1, 2)
     last_sum(0)
     z_step(2, 2)

time: 52.9 us -> 52.5 us (level)
  no operation moved by 1% of the time
where the time goes in v7:
time: 52.5 us; the launch traced here: 52.4 us
  Pallas kernels  51.1 us (97%)
  local copies, waits for them, and re-layouts  0.66 us (1%)
  between operations  0.64 us (1%)
    pallas_call x1, Pallas kernels, per_device(): pl.pallas_call(functools.partial(kernel, nb, nu, n, total, fc), out_shape...  51.1 us

profile of v7, /device:TPU:0, one launch (start us, length us, event | category | flops | bytes accessed | tf_op | source)
XLA Modules:
  0.0 52.4 jit_solution(12536977331959611011)
XLA Ops:
  0.6 51.1 %shard_map.68 = bf16[2,10,2048]{2,1,0:T(8,128)(2,1)S(1)} custom-call(bf16[10,2048]{1,0:T(8,128)(2,1)} %tok_in.1, bf16[10,2048]{1,0:T(8,128)(2,1)} %cot_in.1, bf16[2048,6656]{1,0:T(8,128)(2,1)} %wg_hbm.1, bf16[2048,6656]{1,0:T(8,128)(2,1)} %wu_hbm.1, bf16[6656,2048]{1,0:T(8,128)(2,1)} %wd_hbm.1), custom_call_target="tpu_custom_call" | custom-call | tf_op jit(solution)/shard_map/pallas_call | solution.py:570
  51.7 0.7 %slice_bitcast_fusion = (bf16[10,2048]{1,0:T(8,128)(2,1)}, bf16[10,2048]{1,0:T(8,128)(2,1)}) fusion(bf16[2,10,2048]{2,1,0:T(8,128)(2,1)S(1)} %shard_map.68), kind=kLoop, calls=%fused_computation | loop fusion | bytes 163840 | tf_op jit(solution)/shard_map/squeeze | solution.py:595
